TPU v7x, 32 devices: a whole 2x2x4 slice. The times are simulated.
32 devices in a mesh: group: 4 (over y, x), fsdp: 8 (over z, core).
Axes of the slice: x: 2, y: 2, z: 4, core: 2. Of those that a mesh axis runs over, the one named last changes fastest.
Arguments:
- inputs: bfloat16 [8192, 4096], P('group', 'fsdp'), may hold values from -6 to 6
- norm_gain: bfloat16 [4096], P('fsdp'), may hold values from 0.099609375 to 1.8984375
- cotangent: bfloat16 [8192, 16384], P('group', 'fsdp'), may hold values from -0.03125 to 0.03125
- owners: int32 [32, 4], P('fsdp'), may hold values from 0 to 3, each once within a row
- refresh: int32 [8, 32], P('group', 'fsdp'), may hold values 0 or 1
- left_stats: float32 [4096, 16384], P('group', 'fsdp'), may hold values from -1 to 16, as said below
- right_stats: float32 [4096, 16384], P('group', 'fsdp'), may hold values from -1 to 16, as said below
- left_inverse: float32 [4096, 16384], P('group', 'fsdp'), may hold values from -1 to 8, as said below
- right_inverse: float32 [4096, 16384], P('group', 'fsdp'), may hold values from -1 to 8, as said below
Outputs:
- update: bfloat16 [4096, 16384], P('group', 'fsdp')
- left_accum: float32 [4096, 16384], P('group', 'fsdp')
- right_accum: float32 [4096, 16384], P('group', 'fsdp')
- left_refreshed: float32 [4096, 16384], P('group', 'fsdp')
- right_refreshed: float32 [4096, 16384], P('group', 'fsdp')
Inputs may be any that keep to these rules, and one draw needn't show every extreme that they name: Each row owners[c] is a permutation of 0 to 4 - 1. `left_stats`: symmetric within each 512 x 512 block, diagonal entries at least 1. `right_stats`: symmetric within each 512 x 512 block, diagonal entries at least 1. `left_inverse`: symmetric within each 512 x 512 block. `right_inverse`: symmetric within each 512 x 512 block.
All inputs are finite; a program needn't handle non-finite values. No bound on the sum of `refresh` on one device may be relied on, other than what follows from the above.
Results may differ from a plain program's by a relative error of at most 0.013.
Values may be sent and summed in bfloat16 or wider, within the bound.
A program may use at most 256 MiB of HBM per device.

v0:
```python
import jax
import jax.numpy as jnp
from jax import lax
from jax.experimental import pallas as pl
from jax.experimental.pallas import tpu as pltpu
from jax.sharding import PartitionSpec as P

BLK = 512

NORM_EPSILON = 1e-05
SCALE_EPSILON = 1e-06
DECAY_RATE = 0.95
RIDGE_TERM = 1e-06
C0 = 1.5625
C1 = -0.3125 - 3125.0 / 4096.0
C2 = 3125.0 / 4096.0
C3 = -1250.0 / 4096.0
C4 = 250.0 / 4096.0
C5 = -25.0 / 4096.0
C6 = 1.0 / 4096.0


def dot(a, b, dims=(((1,), (0,)), ((), ()))):
    return lax.dot_general(a, b, dims, preferred_element_type=jnp.float32)


def split(value):
    high = value.astype(jnp.bfloat16)
    return high, (value - high.astype(jnp.float32)).astype(jnp.bfloat16)


def inverse_fourth_root(statistic):
    rows = lax.broadcasted_iota(jnp.int32, statistic.shape, 0)
    cols = lax.broadcasted_iota(jnp.int32, statistic.shape, 1)
    diagonal = rows == cols
    matrix = statistic + jnp.where(diagonal, RIDGE_TERM, 0.0)
    scaling = 2.5 * lax.rsqrt(jnp.sum(matrix * matrix, keepdims=True))
    m1 = scaling * matrix
    m1_low = m1.astype(jnp.bfloat16)
    m2 = dot(m1_low, m1_low)
    m3 = dot(m2.astype(jnp.bfloat16), m1_low)
    upper = dot(
        m3.astype(jnp.bfloat16), (C4 * m1 + C5 * m2 + C6 * m3).astype(jnp.bfloat16)
    )
    total = C1 * m1 + C2 * m2 + C3 * m3 + upper + jnp.where(diagonal, C0, 0.0)
    return jnp.sqrt(jnp.sqrt(scaling)) * total


def block_kernel(chunk, col_blocks, refresh, g_ref, ls_ref, rs_ref, li_ref, ri_ref, *rest):
    upd_ref, la_ref, ra_ref, ln_ref, rn_ref = rest[-5:]
    grad = g_ref[...]
    left_high, left_low = split(li_ref[...])
    half = dot(left_high, grad) + dot(left_low, grad)
    half_high, half_low = split(half)
    right_high, right_low = split(ri_ref[...])
    conditioned = dot(half_high, right_high) + dot(half_low, right_high) + dot(half_high, right_low)
    mean = jnp.sum(conditioned * conditioned, keepdims=True) * (1.0 / conditioned.size)
    upd_ref[...] = (conditioned * lax.rsqrt(mean + SCALE_EPSILON)).astype(jnp.bfloat16)
    la_ref[...] = DECAY_RATE * ls_ref[...] + (1.0 - DECAY_RATE) * dot(
        grad, grad, (((1,), (1,)), ((), ()))
    )
    ra_ref[...] = DECAY_RATE * rs_ref[...] + (1.0 - DECAY_RATE) * dot(
        grad, grad, (((0,), (0,)), ((), ()))
    )
    flag = refresh[pl.program_id(0) * col_blocks + chunk]

    @pl.when(flag > 0)
    def _():
        ln_ref[...] = inverse_fourth_root(la_ref[...])
        rn_ref[...] = inverse_fourth_root(ra_ref[...])

    @pl.when(flag <= 0)
    def _():
        ln_ref[...] = li_ref[...]
        rn_ref[...] = ri_ref[...]


def block_call(chunk, grad, refresh, states, previous):
    slab_rows, local_cols = states[0].shape
    col_blocks = local_cols // BLK
    here = pl.BlockSpec((BLK, BLK), lambda r, flags: (r, chunk))
    own = pl.BlockSpec((BLK, BLK), lambda r, flags: (r, 0))
    held = [pl.BlockSpec(memory_space=pl.ANY)] * len(previous)
    whole = jax.ShapeDtypeStruct((slab_rows, local_cols), jnp.float32)
    steps = slab_rows // BLK

    def kernel(*refs):
        block_kernel(chunk, col_blocks, *refs)

    return pl.pallas_call(
        kernel,
        grid_spec=pltpu.PrefetchScalarGridSpec(
            num_scalar_prefetch=1,
            grid=(steps,),
            in_specs=[own] + [here] * 4 + held,
            out_specs=[own] + [here] * 4,
        ),
        out_shape=[jax.ShapeDtypeStruct((slab_rows, BLK), jnp.bfloat16)] + [whole] * 4,
        input_output_aliases={6 + i: 1 + i for i in range(len(previous))},
        compiler_params=pltpu.CompilerParams(
            dimension_semantics=("arbitrary",), vmem_limit_bytes=48 * 1024 * 1024
        ),
        cost_estimate=pl.CostEstimate(
            flops=steps * 13 * 2 * BLK**3,
            bytes_accessed=steps * 9 * 4 * BLK * BLK,
            transcendentals=0,
        ),
        name="block_step",
    )(refresh, grad, *states, *previous)


def body(
    inputs,
    norm_gain,
    cotangent,
    owners,
    refresh,
    left_stats,
    right_stats,
    left_inverse,
    right_inverse,
):
    my_group = lax.axis_index("group")
    slab_rows, local_cols = left_stats.shape
    col_blocks = local_cols // BLK
    shards = owners.shape[1]
    gathered, gain_whole = (
        lax.all_gather(inputs, "fsdp", axis=1, tiled=True),
        lax.all_gather(norm_gain, "fsdp", axis=0, tiled=True),
    )
    values = gathered.astype(jnp.float32)
    scales = lax.rsqrt(jnp.mean(values * values, axis=1) + NORM_EPSILON)
    normed = (values * scales[:, None] * gain_whole.astype(jnp.float32)[None, :]).astype(
        jnp.bfloat16
    )
    flags = refresh.reshape(-1)
    ranks = jnp.arange(shards, dtype=jnp.int32)
    sources = jnp.sum(
        jnp.where(owners[:, :, None] == ranks[None, None, :], ranks[None, :, None], 0), axis=1
    )
    owner_here = owners[:, my_group]
    states = (left_stats, right_stats, left_inverse, right_inverse)
    owned = []
    for chunk in range(col_blocks):
        partial_value = lax.dot_general(
            normed,
            cotangent[:, chunk * BLK : (chunk + 1) * BLK],
            (((0,), (0,)), ((), ())),
            preferred_element_type=jnp.float32,
        ).astype(jnp.bfloat16)
        placed = jnp.concatenate(
            [
                lax.dynamic_slice(
                    partial_value, (sources[chunk, place] * slab_rows, 0), (slab_rows, BLK)
                )
                for place in range(shards)
            ],
            axis=0,
        )
        owned.append(lax.psum_scatter(placed, "group", scatter_dimension=0, tiled=True))
    previous = ()
    updates = []
    for chunk in range(col_blocks):
        own_update, *previous = block_call(chunk, owned[chunk], flags, states, tuple(previous))
        portion = lax.all_gather(own_update, "group", axis=0, tiled=True)
        updates.append(
            lax.dynamic_slice(portion, (owner_here[chunk] * slab_rows, 0), (slab_rows, BLK))
        )
    return (jnp.concatenate(updates, axis=1), *previous)


def solution(mesh):
    spec = P("group", "fsdp")
    in_specs = (spec, P("fsdp"), spec, P("fsdp", None), spec, spec, spec, spec, spec)
    return jax.shard_map(
        body, mesh=mesh, in_specs=in_specs, out_specs=(spec,) * 5, check_vma=False
    )
```

profile of v0, /device:TPU:0, one launch (start us, length us, event | category | flops | bytes accessed | tf_op | source)
XLA Modules:
  0.0 656.5 jit_solution(14387690755977143757)
XLA Ops:
  12.7 14.5 %all-gather = bf16[8,1,512]{2,1,0:T(2,128)(2,1)S(1)} all-gather(bf16[1,1,512]{2,1,0:T(2,128)(2,1)S(1)} %reshape.69), channel_id=1, replica_groups=mesh['group'=4,'fsdp'=8] {'fsdp'}, dimensions={0}, use_global_device_ids=true | all-gather | bytes 9216 | tf_op jit(solution)/shard_map/all_gather | solution.py:129
  27.2 136.2 %all-gather.7.cloned.1.call-done = bf16[2048,4096]{1,0:T(8,128)(2,1)} async-done(((bf16[2048,512]{1,0:T(8,128)(2,1)}), bf16[2048,4096]{1,0:T(8,128)(2,1)}) %all-gather.7.cloned.1.call-update) | async-done | bytes 16777232 | tf_op jit(solution)/shard_map/all_gather | solution.py:128
  163.4 7.5 %fusion = f32[2048]{0:T(1024)S(1)} fusion(bf16[2048,4096]{1,0:T(8,128)(2,1)} %all-gather.7.cloned.1.call-done), kind=kLoop, calls=%fused_computation.2 | loop fusion | flops 25163776 | bytes 16785408 | tf_op jit(solution)/shard_map/reduce_sum | solution.py:132
  170.9 3.2 copy-done.4
  174.1 17.4 %convolution_convert_fusion.3 = bf16[4096,512]{1,0:T(8,128)(2,1)} fusion(bf16[2048,2048]{1,0:T(8,128)(2,1)} %param.11, bf16[2048,4096]{1,0:T(8,128)(2,1)S(1)} %copy-done.4, f32[4096]{0:T(1024)S(1)} %bitcast.21, f32[2048]{0:T(1024)S(1)} %add_rsqrt_fusion), kind=kOutput, calls=%fused_computation.8 | convolution fusion | flops 8625586176 | bytes 23093248 | tf_op jit(solution)/shard_map/dot_general | solution.py:145
  191.5 2.4 constant_dynamic-slice_fusion.20
  193.9 2.2 pad_maximum_fusion
  198.8 15.1 %convolution_convert_fusion.2 = bf16[4096,512]{1,0:T(8,128)(2,1)S(1)} fusion(bf16[2048,2048]{1,0:T(8,128)(2,1)} %param.11, bf16[2048,4096]{1,0:T(8,128)(2,1)} %all-gather.7.cloned.1.call-done, f32[4096]{0:T(1024)S(1)} %bitcast.22, f32[2048]{0:T(1024)S(1)} %add_rsqrt_fusion), kind=kOutput, calls=%fused_computation.7 | convolution fusion | flops 8625586176 | bytes 23093248 | tf_op jit(solution)/shard_map/dot_general | solution.py:145
  214.2 2.2 pad_maximum_fusion.1
  219.0 14.5 %convolution_convert_fusion.1 = bf16[4096,512]{1,0:T(8,128)(2,1)S(1)} fusion(bf16[2048,2048]{1,0:T(8,128)(2,1)} %param.11, bf16[2048,4096]{1,0:T(8,128)(2,1)} %all-gather.7.cloned.1.call-done, f32[4096]{0:T(1024)S(1)} %bitcast.23, f32[2048]{0:T(1024)S(1)} %add_rsqrt_fusion), kind=kOutput, calls=%fused_computation.6 | convolution fusion | flops 8625586176 | bytes 23093248 | tf_op jit(solution)/shard_map/dot_general | solution.py:145
  233.8 2.2 pad_maximum_fusion.2
  238.9 14.5 %convolution_convert_fusion = bf16[4096,512]{1,0:T(8,128)(2,1)S(1)} fusion(bf16[2048,2048]{1,0:T(8,128)(2,1)} %param.11, bf16[2048,4096]{1,0:T(8,128)(2,1)} %all-gather.7.cloned.1.call-done, f32[4096]{0:T(1024)S(1)} %bitcast.24, f32[2048]{0:T(1024)S(1)} %add_rsqrt_fusion), kind=kOutput, calls=%fused_computation.5 | convolution fusion | flops 8625586176 | bytes 23093248 | tf_op jit(solution)/shard_map/dot_general | solution.py:145
  257.6 12.5 %block_step.4 = (bf16[1024,512]{1,0:T(8,128)(2,1)}, f32[1024,2048]{1,0:T(8,128)}, f32[1024,2048]{1,0:T(8,128)}, f32[1024,2048]{1,0:T(8,128)}, f32[1024,2048]{1,0:T(8,128)}) custom-call(s32[8]{0:T(128)S(1)} %reshape.68.refs_0_, bf16[1024,512]{1,0:T(8,128)(2,1)S(1)} %copy-done.3, f32[1024,2048]{1,0:T(8,128)} %refs_2_.7, f32[1024,2048]{1,0:T(8,128)} %refs_3_.7, ...), custom_call_target="tpu_custom_call" | custom-call | flops 6979321856 | bytes 18874368 | tf_op jit(solution)/shard_map/block_step/pallas_call | solution.py:90
  270.1 32.6 %reduce-scatter.7.cloned.1.call-done.refs_1_ = bf16[1024,512]{1,0:T(8,128)(2,1)} async-done(((bf16[4096,512]{1,0:T(8,128)(2,1)}), bf16[1024,512]{1,0:T(8,128)(2,1)}) %reduce-scatter.7.cloned.1.call-update) | async-done | bytes 1048592 | tf_op jit(solution)/shard_map/reduce_scatter | solution.py:160
  303.9 15.3 %block_step.5 = (bf16[1024,512]{1,0:T(8,128)(2,1)}, f32[1024,2048]{1,0:T(8,128)}, f32[1024,2048]{1,0:T(8,128)}, f32[1024,2048]{1,0:T(8,128)}, f32[1024,2048]{1,0:T(8,128)}) custom-call(s32[8]{0:T(128)S(1)} %reshape.68.refs_0_, bf16[1024,512]{1,0:T(8,128)(2,1)S(1)} %copy-done, ...), custom_call_target="tpu_custom_call", output_to_operand_aliasing={{1}: (6, {}), {2}: (7, {}), {3}: (8, {}), {4}: (9, {})} | custom-call | flops 6979321856 | bytes 18874368 | tf_op jit(solution)/shard_map/block_step/pallas_call | solution.py:90
  319.3 38.9 %reduce-scatter.9.cloned.1.call-done.refs_1_ = bf16[1024,512]{1,0:T(8,128)(2,1)} async-done(((bf16[4096,512]{1,0:T(8,128)(2,1)}), bf16[1024,512]{1,0:T(8,128)(2,1)}) %reduce-scatter.9.cloned.1.call-update) | async-done | bytes 1048592 | tf_op jit(solution)/shard_map/reduce_scatter | solution.py:160
  359.4 12.7 %block_step.6 = (bf16[1024,512]{1,0:T(8,128)(2,1)}, f32[1024,2048]{1,0:T(8,128)}, f32[1024,2048]{1,0:T(8,128)}, f32[1024,2048]{1,0:T(8,128)}, f32[1024,2048]{1,0:T(8,128)}) custom-call(s32[8]{0:T(128)S(1)} %reshape.68.refs_0_, bf16[1024,512]{1,0:T(8,128)(2,1)S(1)} %copy-done.1, ...), custom_call_target="tpu_custom_call", output_to_operand_aliasing={{1}: (6, {}), {2}: (7, {}), {3}: (8, {}), {4}: (9, {})} | custom-call | flops 6979321856 | bytes 18874368 | tf_op jit(solution)/shard_map/block_step/pallas_call | solution.py:90
  372.1 42.1 %reduce-scatter.11.cloned.1.call-done.refs_1_ = bf16[1024,512]{1,0:T(8,128)(2,1)} async-done(((bf16[4096,512]{1,0:T(8,128)(2,1)}), bf16[1024,512]{1,0:T(8,128)(2,1)}) %reduce-scatter.11.cloned.1.call-update) | async-done | bytes 1048592 | tf_op jit(solution)/shard_map/reduce_scatter | solution.py:160
  415.4 12.5 %block_step.7 = (bf16[1024,512]{1,0:T(8,128)(2,1)}, f32[1024,2048]{1,0:T(8,128)}, f32[1024,2048]{1,0:T(8,128)}, f32[1024,2048]{1,0:T(8,128)}, f32[1024,2048]{1,0:T(8,128)}) custom-call(s32[8]{0:T(128)S(1)} %reshape.68.refs_0_, bf16[1024,512]{1,0:T(8,128)(2,1)S(1)} %copy-done.2, ...), custom_call_target="tpu_custom_call", output_to_operand_aliasing={{1}: (6, {}), {2}: (7, {}), {3}: (8, {}), {4}: (9, {})} | custom-call | flops 6979321856 | bytes 18874368 | tf_op jit(solution)/shard_map/block_step/pallas_call | solution.py:90
  433.4 49.2 %all-gather.15.cloned.1.call-done = bf16[4096,512]{1,0:T(8,128)(2,1)} async-done(((bf16[1024,512]{1,0:T(8,128)(2,1)}), bf16[4096,512]{1,0:T(8,128)(2,1)}) %all-gather.15.cloned.1.call-update) | async-done | bytes 4194320 | tf_op jit(solution)/shard_map/all_gather | solution.py:165
  483.9 53.1 %all-gather.13.cloned.1.call-done = bf16[4096,512]{1,0:T(8,128)(2,1)} async-done(((bf16[1024,512]{1,0:T(8,128)(2,1)}), bf16[4096,512]{1,0:T(8,128)(2,1)}) %all-gather.13.cloned.1.call-update) | async-done | bytes 4194320 | tf_op jit(solution)/shard_map/all_gather | solution.py:165
  538.3 53.1 %all-gather.11.cloned.1.call-done = bf16[4096,512]{1,0:T(8,128)(2,1)} async-done(((bf16[1024,512]{1,0:T(8,128)(2,1)}), bf16[4096,512]{1,0:T(8,128)(2,1)}) %all-gather.11.cloned.1.call-update) | async-done | bytes 4194320 | tf_op jit(solution)/shard_map/all_gather | solution.py:165
  592.8 53.2 %all-gather.9.cloned.1.call-done = bf16[4096,512]{1,0:T(8,128)(2,1)} async-done(((bf16[1024,512]{1,0:T(8,128)(2,1)}), bf16[4096,512]{1,0:T(8,128)(2,1)}) %all-gather.9.cloned.1.call-update) | async-done | bytes 4194320 | tf_op jit(solution)/shard_map/all_gather | solution.py:165
  647.2 2.3 pad_maximum_fusion.4
  (48 shorter events, 19.9 us)
Async XLA Ops:
  7.2 156.3 %all-gather.7.cloned.1.call-start = ((), (), s32[]{:S(2)}) async-start(), calls=%async_computation.4 | async-start | bytes 18874368 | tf_op jit(solution)/shard_map/all_gather | solution.py:128
  7.9 248.2 %reduce-scatter.5.cloned.1.call-start = ((), (), s32[]{:S(2)}) async-start(), calls=%async_computation.5 | async-start | bytes 5242880 | tf_op jit(solution)/shard_map/reduce_scatter | solution.py:160
  163.4 10.7 %copy-start.4 = (bf16[2048,4096]{1,0:T(8,128)(2,1)S(1)}, bf16[2048,4096]{1,0:T(8,128)(2,1)}, u32[]{:S(2)}) copy-start(bf16[2048,4096]{1,0:T(8,128)(2,1)} %all-gather.7.cloned.1.call-done) | copy-start | bytes 50331652
  196.1 106.6 %reduce-scatter.7.cloned.1.call-start = ((), (), s32[]{:S(2)}) async-start(), calls=%async_computation.7 | async-start | bytes 5242880 | tf_op jit(solution)/shard_map/reduce_scatter | solution.py:160
  216.5 141.7 %reduce-scatter.9.cloned.1.call-start = ((), (), s32[]{:S(2)}) async-start(), calls=%async_computation.9 | async-start | bytes 5242880 | tf_op jit(solution)/shard_map/reduce_scatter | solution.py:160
  236.1 178.1 %reduce-scatter.11.cloned.1.call-start = ((), (), s32[]{:S(2)}) async-start(), calls=%async_computation.11 | async-start | bytes 5242880 | tf_op jit(solution)/shard_map/reduce_scatter | solution.py:160
  253.7 2.3 copy-start.6
  255.9 226.7 %all-gather.15.cloned.1.call-start = ((), (), s32[]{:S(2)}) async-start(), calls=%async_computation.12 | async-start | bytes 5242880 | tf_op jit(solution)/shard_map/all_gather | solution.py:165
  256.1 1.5 copy-start.3
  302.7 1.2 copy-start
  358.2 1.2 copy-start.1
  414.2 1.2 copy-start.2
  415.4 14.8 %copy-start.5 = (s32[4,4]{1,0:T(4,128)S(1)}, s32[4,4]{1,0:T(4,128)}, u32[]{:S(2)}) copy-start(s32[4,4]{1,0:T(4,128)} %param.12) | copy-start | bytes 196
  428.0 109.1 %all-gather.13.cloned.1.call-start = ((), (), s32[]{:S(2)}) async-start(), calls=%async_computation.10 | async-start | bytes 5242880 | tf_op jit(solution)/shard_map/all_gather | solution.py:165
  428.7 162.8 %all-gather.11.cloned.1.call-start = ((), (), s32[]{:S(2)}) async-start(), calls=%async_computation.8 | async-start | bytes 5242880 | tf_op jit(solution)/shard_map/all_gather | solution.py:165
  429.5 216.5 %all-gather.9.cloned.1.call-start = ((), (), s32[]{:S(2)}) async-start(), calls=%async_computation.6 | async-start | bytes 5242880 | tf_op jit(solution)/shard_map/all_gather | solution.py:165
Sparse Core Ops, SparseCore 0:
  9.6 153.7 all-gather.6
  196.2 50.8 reduce-scatter.4
  250.1 52.5 reduce-scatter.6
  305.5 52.5 reduce-scatter.8
  361.6 52.5 reduce-scatter.10
  428.1 54.4 all-gather.14
  484.4 52.5 all-gather.12
  538.9 52.5 all-gather.10
  593.3 52.5 all-gather.8
where the time goes:
time: 662 us; the launch traced here: 657 us
  waiting for transfers between devices  461 us (70%)
  matrix products  61.6 us (9%)
  Pallas kernels  53.1 us (8%)
  between operations  27 us (4%)
  other arithmetic  19.4 us (3%)
  local copies, waits for them, and re-layouts  19 us (3%)
  blocking collectives  14.5 us (2%)
    all_gather x4, waiting for transfers between devices, body(): portion = lax.all_gather(own_update, 'group', axis=0, tiled=True)  209 us
    all_gather x1, waiting for transfers between devices, body(): lax.all_gather(inputs, 'fsdp', axis=1, tiled=True)  136 us
    reduce_scatter x4, waiting for transfers between devices, body(): lax.psum_scatter(placed, 'group', scatter_dimension=0, tiled=True)  114 us
    dot_general x4, matrix products, body(): lax.dot_general(normed, cotangent[:, chunk * BLK:(chunk + 1) * BLK], (((0...  61.6 us
    pallas_call x4, Pallas kernels, block_call(): pl.pallas_call(kernel, grid_spec=pltpu.PrefetchScalarGridSpec(num_scalar_...  53.1 us
    all_gather x1, blocking collectives, body(): lax.all_gather(norm_gain, 'fsdp', axis=0, tiled=True)  14.5 us
  transfers between devices with their start and end apart: 9, of which 8 were waited for; matrix products, arithmetic and copies ran while one was open for 9% of the time, Pallas kernels for 6%

commit v1 on v0

v1 whole, which is shorter than its diff:
```python
import functools
import jax
import jax.numpy as jnp
from jax import lax
from jax.experimental import pallas as pl
from jax.experimental.pallas import tpu as pltpu
from jax.sharding import PartitionSpec as P

BLK = 512
NORM_EPSILON = 1e-05
MESH = pl.DeviceIdType.MESH
RING = 4


def remote(src, dst, send_sem, recv_sem, device):
    return pltpu.make_async_remote_copy(
        src_ref=src, dst_ref=dst, send_sem=send_sem, recv_sem=recv_sem,
        device_id=device, device_id_type=MESH,
    )


def grad_kernel(G, F, NC, LEAD, TN, owners, gain, x_hbm, cot_hbm, og, xbuf, xt, gcol, cotv, ga, ssall, res, *rest):
    nb = G.bit_length() - 1
    sends, recvs, curs = rest[:nb], rest[nb:2 * nb], rest[2 * nb:3 * nb - 1]
    lsem, ss_send, ss_recv, gs, gl, gr, rs_send, rs_recv = rest[3 * nb - 1:]
    T, S = xbuf.shape
    N = cotv.shape[1]
    D = S * F
    L, q, rk, Nh = F // 2, F // G, S // NC, N // 2
    R, M = q * rk, F * rk
    W = min(BLK, Nh)
    g, f = lax.axis_index("group"), lax.axis_index("fsdp")
    l, core = f // 2, f % 2
    sib = f + 1 - 2 * core

    def bit(b):
        return (g // (1 << b)) % 2

    def partner(b):
        return g + (1 - 2 * bit(b)) * (1 << b)

    x_copy = pltpu.make_async_copy(x_hbm, xbuf, lsem.at[0])
    x_copy.start()
    cot_copy = pltpu.make_async_copy(cot_hbm, cotv, lsem.at[1])
    cot_copy.start()

    barrier = pltpu.get_barrier_semaphore()
    for d in range(1, F):
        pl.semaphore_signal(barrier, inc=1, device_id=(g, (f + d) % F), device_id_type=MESH)
    for b in range(nb):
        pl.semaphore_signal(barrier, inc=1, device_id=(partner(b), f), device_id_type=MESH)

    gcol[...] = jnp.broadcast_to(gain[...].astype(jnp.float32), (128, S)).T
    x_copy.wait()
    TT = 256
    for i in range(T // TT):
        v = xbuf[i * TT:(i + 1) * TT, :].astype(jnp.float32).T
        ssall[f, :, i * TT:(i + 1) * TT] = jnp.sum(v * v, axis=0, keepdims=True)
        xt[:, i * TT:(i + 1) * TT] = v.astype(jnp.bfloat16)
    pl.semaphore_wait(barrier, F - 1 + nb)

    def ss_copy(slot, peer, d):
        return remote(ssall.at[slot], ssall.at[slot], ss_send.at[d - 1], ss_recv.at[slot], (g, peer))

    for d in range(1, F):
        ss_copy(f, (f + d) % F, d).start()
    for d in range(1, F):
        peer = (f + d) % F
        ss_copy(peer, peer, d).wait_recv()
    total = jnp.sum(ssall[...], axis=0)
    scale = lax.rsqrt(total * (1.0 / D) + NORM_EPSILON)

    def piece(k, shard, send_sem, peer):
        return remote(ga.at[k, shard], ga.at[k, shard], send_sem, gr.at[k, shard], (g, peer))

    def onward(k, src, go, peer, then):
        shard, ring = 2 * src + core, k % RING

        @pl.when(go)
        def _():
            then(piece(k, shard, gs.at[ring, src, 0], peer))

        then(piece(k, shard, gs.at[ring, src, 1], sib))

    def own(k, then):
        onward(k, l, l < L - 1, f + 2, then)

        @pl.when(l > 0)
        def _():
            then(piece(k, f, gl.at[k % RING], f - 2))

    def forward(k, d, then, receive):
        @pl.when(l - d >= 0)
        def _():
            if receive:
                piece(k, 2 * (l - d) + core, gs.at[0, 0, 0], sib).wait_recv()
            onward(k, l - d, l < L - 1, f + 2, then)

        @pl.when(l + d <= L - 1)
        def _():
            if receive:
                piece(k, 2 * (l + d) + core, gs.at[0, 0, 0], sib).wait_recv()
            onward(k, l + d, l > 0, f - 2, then)

    def start(copy):
        copy.start()

    def finish(copy):
        copy.wait_send()

    def wait_sibling(k):
        for src in range(L):
            piece(k, 2 * src + 1 - core, gs.at[0, 0, 0], sib).wait_recv()

    def drain_gather(k):
        own(k, finish)
        for d in range(1, L):
            forward(k, d, finish, False)

    def normalize(k, _):
        rows = pl.ds(pl.multiple_of(k * rk, rk), rk)
        v = xt[rows, :].astype(jnp.float32) * scale * gcol[rows, :1]
        ga[k, f] = v.astype(jnp.bfloat16)

        @pl.when(k <= LEAD)
        def _():
            own(k, start)

        return 0

    lax.fori_loop(0, NC, normalize, 0)
    for k in range(LEAD):
        for d in range(1, L):
            forward(k, d, start, True)
    cot_copy.wait()

    def slab_at(c, place):
        found = jnp.int32(0)
        for s in range(1, G):
            found = jnp.where(owners[c, s] == place, s, found)
        return found

    def order(h):
        return list(range(nb)) if h == 0 else list(range(nb))[::-1]

    def place_of(h, i, flip, j):
        bits = order(h)
        place = jnp.int32(0)
        for m in range(i + 1):
            mine = bit(bits[m])
            place = place + (1 - mine if (flip and m == i) else mine) * (1 << bits[m])
        left = bits[i + 1:]
        for m, b in enumerate(left):
            place = place + ((j // (1 << (len(left) - 1 - m))) % 2) * (1 << b)
        return place

    def exchange(k, h, i):
        return remote(sends[i].at[k % 2, h], recvs[i].at[k, h], rs_send.at[i, k % 2, h], rs_recv.at[i, k, h],
                      (partner(order(h)[i]), f))

    def reuse(k, h, i):
        @pl.when(k >= 2)
        def _():
            exchange(k - 2, h, i).wait_send()

    def segments(h):
        for n in range(Nh // W):
            yield (h * Nh + n * W) // BLK, h * Nh + n * W, n * W

    def first_send(k):
        for h in range(2):
            reuse(k, h, 0)
            for j in range(G // 2):
                place = place_of(h, 0, True, j)
                for c, col, at in segments(h):
                    sends[0][k % 2, h, j, :, at:at + W] = res[k % 2, slab_at(c, place), :, col:col + W]
            exchange(k, h, 0).start()

    def receive(k, i):
        for h in range(2):
            exchange(k, h, i).wait_recv()
            if i == nb - 1:
                for c, col, at in segments(h):
                    if i == 0:
                        v = res[k % 2, slab_at(c, g), :, col:col + W].astype(jnp.float32)
                    else:
                        v = curs[i - 1][h, 0, :, at:at + W]
                    v = (v + recvs[i][k, h, 0, :, at:at + W].astype(jnp.float32)).astype(jnp.bfloat16)
                    for m in range(q):
                        og[pl.ds(pl.multiple_of(m * S + k * rk, rk), rk), col:col + W] = v[m * rk:(m + 1) * rk]
                continue
            reuse(k, h, i + 1)
            count = 1 << (nb - i - 2)
            mine = bit(order(h)[i + 1])
            for keep in (0, 1):
                side = mine if keep else 1 - mine
                for j in range(count):
                    at_j = side * count + j
                    place = place_of(h, i, False, at_j)
                    for c, col, at in segments(h):
                        if i == 0:
                            v = res[k % 2, slab_at(c, place), :, col:col + W].astype(jnp.float32)
                        else:
                            v = curs[i - 1][h, at_j, :, at:at + W]
                        v = v + recvs[i][k, h, at_j, :, at:at + W].astype(jnp.float32)
                        if keep:
                            curs[i][h, j, :, at:at + W] = v
                        else:
                            sends[i + 1][k % 2, h, j, :, at:at + W] = v.astype(jnp.bfloat16)
                if not keep:
                    exchange(k, h, i + 1).start()

    def step(t, _):
        @pl.when(t < NC)
        def _():
            wait_sibling(t)

            @pl.when(t >= RING - 1 - LEAD)
            def _():
                drain_gather(t + LEAD + 1 - RING)

            @pl.when(t + LEAD < NC)
            def _():
                forward(t + LEAD, 1, start, True)

            def tile(n, _):
                cols = pl.ds(pl.multiple_of(n * TN, TN), TN)
                v = jnp.dot(ga[t].reshape(M, T), cotv[:, cols], preferred_element_type=jnp.float32)
                res[t % 2, :, :, cols] = v.astype(jnp.bfloat16).reshape(G, R, TN)
                return 0

            lax.fori_loop(0, N // TN, tile, 0)
            first_send(t)

        for i in range(nb - 1, -1, -1):
            @pl.when((t - 1 - i >= 0) & (t - 1 - i < NC))
            def _():
                receive(t - 1 - i, i)

        @pl.when(t + LEAD < NC)
        def _():
            for d in range(2, L):
                forward(t + LEAD, d, start, True)

        @pl.when(t + LEAD + 1 < NC)
        def _():
            own(t + LEAD + 1, start)

        return 0

    lax.fori_loop(0, NC + nb, step, 0)
    for d in range(1, F):
        ss_copy(f, (f + d) % F, d).wait_send()
    for k in range(NC + LEAD + 1 - RING, NC):
        drain_gather(k)
    for i in range(nb):
        for h in range(2):
            for k in (NC - 2, NC - 1):
                exchange(k, h, i).wait_send()


def gradient(G, F, owners, gain, x, cot, NC=8, LEAD=1, TN=1024):
    NC = min(NC, x.shape[1] // 16)
    TN = min(TN, cot.shape[1])
    T, S = x.shape
    N = cot.shape[1]
    nb = G.bit_length() - 1
    L, q, rk, Nh = F // 2, F // G, S // NC, N // 2
    R = q * rk
    slab = S * F // G
    bf, f32 = jnp.bfloat16, jnp.float32
    counts = [G >> (i + 1) for i in range(nb)]
    dma = pltpu.SemaphoreType.DMA
    return pl.pallas_call(
        functools.partial(grad_kernel, G, F, NC, LEAD, TN),
        out_shape=jax.ShapeDtypeStruct((slab, N), bf),
        in_specs=[
            pl.BlockSpec(memory_space=pltpu.SMEM),
            pl.BlockSpec(memory_space=pltpu.VMEM),
            pl.BlockSpec(memory_space=pl.ANY),
            pl.BlockSpec(memory_space=pl.ANY),
        ],
        out_specs=pl.BlockSpec(memory_space=pltpu.VMEM),
        scratch_shapes=[
            pltpu.VMEM((T, S), bf),
            pltpu.VMEM((S, T), bf),
            pltpu.VMEM((S, 128), f32),
            pltpu.VMEM((T, N), bf),
            pltpu.VMEM((NC, F, rk, T), bf),
            pltpu.VMEM((F, 1, T), f32),
            pltpu.VMEM((2, G, R, N), bf),
        ]
        + [pltpu.VMEM((2, 2, n, R, Nh), bf) for n in counts]
        + [pltpu.VMEM((NC, 2, n, R, Nh), bf) for n in counts]
        + [pltpu.VMEM((2, n, R, Nh), f32) for n in counts[1:]]
        + [
            dma((2,)),
            dma((F - 1,)),
            dma((F,)),
            dma((RING, L, 2)),
            dma((RING,)),
            dma((NC, F)),
            dma((nb, 2, 2)),
            dma((nb, NC, 2)),
        ],
        compiler_params=pltpu.CompilerParams(
            collective_id=0, has_side_effects=True, vmem_limit_bytes=62 * 1024 * 1024
        ),
        cost_estimate=pl.CostEstimate(flops=2 * T * S * F * N, bytes_accessed=2 * (T * S + T * N + slab * N), transcendentals=0),
        name="gradient_step",
    )(owners, gain.reshape(1, S), x, cot)


SCALE_EPSILON = 1e-06
DECAY_RATE = 0.95
RIDGE_TERM = 1e-06
C0 = 1.5625
C1 = -0.3125 - 3125.0 / 4096.0
C2 = 3125.0 / 4096.0
C3 = -1250.0 / 4096.0
C4 = 250.0 / 4096.0
C5 = -25.0 / 4096.0
C6 = 1.0 / 4096.0


def dot(a, b, dims=(((1,), (0,)), ((), ()))):
    return lax.dot_general(a, b, dims, preferred_element_type=jnp.float32)


def split(value):
    high = value.astype(jnp.bfloat16)
    return high, (value - high.astype(jnp.float32)).astype(jnp.bfloat16)


def inverse_fourth_root(statistic):
    rows = lax.broadcasted_iota(jnp.int32, statistic.shape, 0)
    cols = lax.broadcasted_iota(jnp.int32, statistic.shape, 1)
    diagonal = rows == cols
    matrix = statistic + jnp.where(diagonal, RIDGE_TERM, 0.0)
    scaling = 2.5 * lax.rsqrt(jnp.sum(matrix * matrix, keepdims=True))
    m1 = scaling * matrix
    m1_low = m1.astype(jnp.bfloat16)
    m2 = dot(m1_low, m1_low)
    m3 = dot(m2.astype(jnp.bfloat16), m1_low)
    upper = dot(
        m3.astype(jnp.bfloat16), (C4 * m1 + C5 * m2 + C6 * m3).astype(jnp.bfloat16)
    )
    total = C1 * m1 + C2 * m2 + C3 * m3 + upper + jnp.where(diagonal, C0, 0.0)
    return jnp.sqrt(jnp.sqrt(scaling)) * total


def condition_kernel(G, g_ref, li_ref, ri_ref, *rest):
    outs, held = rest[:G], rest[G]
    me = lax.axis_index("group")
    grad = g_ref[...]
    left_high, left_low = split(li_ref[...])
    half = dot(left_high, grad) + dot(left_low, grad)
    half_high, half_low = split(half)
    right_high, right_low = split(ri_ref[...])
    conditioned = dot(half_high, right_high) + dot(half_low, right_high) + dot(half_high, right_low)
    mean = jnp.sum(conditioned * conditioned, keepdims=True) * (1.0 / conditioned.size)
    held[...] = (conditioned * lax.rsqrt(mean + SCALE_EPSILON)).astype(jnp.bfloat16)
    rows = BLK // G
    for m in range(G):
        outs[m][...] = held[pl.ds(pl.multiple_of((me ^ m) * rows, rows), rows), :]


def condition(G, r, grad, left, right):
    N = grad.shape[1]
    here = pl.BlockSpec((BLK, BLK), lambda c: (r, c))
    part = pl.BlockSpec((BLK // G, BLK), lambda c: (0, c))
    return pl.pallas_call(
        functools.partial(condition_kernel, G),
        grid=(N // BLK,),
        in_specs=[here] * 3,
        out_specs=[part] * G,
        out_shape=[jax.ShapeDtypeStruct((BLK // G, N), jnp.bfloat16)] * G,
        scratch_shapes=[pltpu.VMEM((BLK, BLK), jnp.bfloat16)],
        compiler_params=pltpu.CompilerParams(
            dimension_semantics=("arbitrary",), vmem_limit_bytes=40 * 1024 * 1024
        ),
        cost_estimate=pl.CostEstimate(
            flops=(N // BLK) * 5 * 2 * BLK**3, bytes_accessed=(N // BLK) * 12 * BLK * BLK, transcendentals=0
        ),
        name="condition_step",
    )(grad, left, right)


def stats_kernel(r, col_blocks, refresh, g_ref, ls_ref, rs_ref, li_ref, ri_ref, *rest):
    la_ref, ra_ref, ln_ref, rn_ref = rest[-4:]
    grad = g_ref[...]
    la_ref[...] = DECAY_RATE * ls_ref[...] + (1.0 - DECAY_RATE) * dot(
        grad, grad, (((1,), (1,)), ((), ()))
    )
    ra_ref[...] = DECAY_RATE * rs_ref[...] + (1.0 - DECAY_RATE) * dot(
        grad, grad, (((0,), (0,)), ((), ()))
    )
    flag = refresh[r * col_blocks + pl.program_id(0)]

    @pl.when(flag > 0)
    def _():
        ln_ref[...] = inverse_fourth_root(la_ref[...])
        rn_ref[...] = inverse_fourth_root(ra_ref[...])

    @pl.when(flag <= 0)
    def _():
        ln_ref[...] = li_ref[...]
        rn_ref[...] = ri_ref[...]


def stats(r, grad, refresh, states, previous):
    slab_rows, N = states[0].shape
    col_blocks = N // BLK
    here = pl.BlockSpec((BLK, BLK), lambda c, flags: (r, c))
    held = [pl.BlockSpec(memory_space=pl.ANY)] * len(previous)
    whole = jax.ShapeDtypeStruct((slab_rows, N), jnp.float32)
    return pl.pallas_call(
        functools.partial(stats_kernel, r, col_blocks),
        grid_spec=pltpu.PrefetchScalarGridSpec(
            num_scalar_prefetch=1,
            grid=(col_blocks,),
            in_specs=[here] * 5 + held,
            out_specs=[here] * 4,
        ),
        out_shape=[whole] * 4,
        input_output_aliases={6 + i: i for i in range(len(previous))},
        compiler_params=pltpu.CompilerParams(
            dimension_semantics=("arbitrary",), vmem_limit_bytes=48 * 1024 * 1024
        ),
        cost_estimate=pl.CostEstimate(
            flops=col_blocks * 8 * 2 * BLK**3,
            bytes_accessed=col_blocks * 9 * 4 * BLK * BLK,
            transcendentals=0,
        ),
        name="stats_step",
    )(refresh, grad, *states, *previous)


def relay_kernel(G, owners, *refs):
    ins, outs = refs[:G], refs[G:]
    me = lax.axis_index("group")
    c = pl.program_id(0)
    for m in range(G):
        wanted = owners[c * G + (me ^ m)] ^ me
        for k in range(G):
            @pl.when(wanted == k)
            def _():
                outs[m][...] = ins[k][...]


def relay(G, owners, parts):
    rows, N = parts[0].shape
    part = pl.BlockSpec((rows, BLK), lambda c, own: (0, c))
    return pl.pallas_call(
        functools.partial(relay_kernel, G),
        grid_spec=pltpu.PrefetchScalarGridSpec(
            num_scalar_prefetch=1, grid=(N // BLK,), in_specs=[part] * G, out_specs=[part] * G
        ),
        out_shape=[jax.ShapeDtypeStruct((rows, N), jnp.bfloat16)] * G,
        compiler_params=pltpu.CompilerParams(dimension_semantics=("arbitrary",)),
        cost_estimate=pl.CostEstimate(flops=0, bytes_accessed=4 * G * rows * N, transcendentals=0),
        name="relay_step",
    )(owners, *parts)


def place_kernel(G, *refs):
    ins, out = refs[:G], refs[-1]
    me = lax.axis_index("group")
    rows = BLK // G
    for m in range(G):
        out[pl.ds(pl.multiple_of((me ^ m) * rows, rows), rows), :] = ins[m][...]


def place(G, r, slab_rows, parts, previous):
    rows, N = parts[0].shape
    part = pl.BlockSpec((rows, BLK), lambda c: (0, c))
    return pl.pallas_call(
        functools.partial(place_kernel, G),
        grid=(N // BLK,),
        in_specs=[part] * G + [pl.BlockSpec(memory_space=pl.ANY)] * len(previous),
        out_specs=pl.BlockSpec((BLK, BLK), lambda c: (r, c)),
        out_shape=jax.ShapeDtypeStruct((slab_rows, N), jnp.bfloat16),
        input_output_aliases={G: 0} if previous else {},
        compiler_params=pltpu.CompilerParams(dimension_semantics=("arbitrary",)),
        cost_estimate=pl.CostEstimate(flops=0, bytes_accessed=4 * BLK * N, transcendentals=0),
        name="place_step",
    )(*parts, *previous)


def swap(G, parts):
    return [parts[0]] + [
        lax.ppermute(parts[m], "group", [(i, i ^ m) for i in range(G)]) for m in range(1, G)
    ]


def body(G, F, inputs, norm_gain, cotangent, owners, refresh, *states):
    slab_rows, N = states[0].shape
    own = gradient(G, F, owners, norm_gain, inputs, cotangent)
    flat_owners = owners.reshape(-1)
    count = slab_rows // BLK
    sent = [swap(G, condition(G, r, own, states[2], states[3])) for r in range(count)]
    previous = ()
    back = []
    for r in range(count):
        previous = tuple(stats(r, own, refresh.reshape(-1), states, previous))
        back.append(swap(G, relay(G, flat_owners, sent[r])))
    update = ()
    for r in range(count):
        update = (place(G, r, slab_rows, back[r], update),)
    return (*update, *previous)


def solution(mesh):
    spec = P("group", "fsdp")
    in_specs = (spec, P("fsdp"), spec, P("fsdp", None), spec, spec, spec, spec, spec)
    return jax.shard_map(
        functools.partial(body, mesh.shape["group"], mesh.shape["fsdp"]),
        mesh=mesh, in_specs=in_specs, out_specs=(spec,) * 5, check_vma=False
    )
```

time: 662 us -> 309 us (0.47)
  waiting for transfers between devices: 461 us -> 15 us
  Pallas kernels: 53.1 us -> 267 us
  matrix products: 61.6 us -> 0 us
  between operations: 27 us -> 0.79 us
  other arithmetic: 19.4 us -> 0 us
  blocking collectives: 14.5 us -> 0 us
  starting transfers between devices: 0.75 us -> 13.3 us
    all_gather x5 -> x0, waiting for transfers between devices: 345 us -> none  [the longest x4 209 us: body(): portion = lax.all_gather(own_update, 'group', axis=0, tiled=True)]
    pallas_call x4 -> x9, Pallas kernels: 53.1 us -> 267 us  [the longest x1 193 us: gradient(): pl.pallas_call(functools.partial(grad_kernel, G, F, NC, LEAD, TN), out_sh...]
    reduce_scatter x4 -> x0, waiting for transfers between devices: 114 us -> none  [body(): lax.psum_scatter(placed, 'group', scatter_dimension=0, tiled=True)]
    dot_general x4 -> x0, matrix products: 61.6 us -> none  [body(): lax.dot_general(normed, cotangent[:, chunk * BLK:(chunk + 1) * BLK], (((0...]
    ppermute x0 -> x12, waiting for transfers between devices: none -> 15 us  [swap(): lax.ppermute(parts[m], 'group', [(i, i ^ m) for i in range(G)])]
    all_gather x1 -> x0, blocking collectives: 14.5 us -> none  [body(): lax.all_gather(norm_gain, 'fsdp', axis=0, tiled=True)]
    ppermute x0 -> x12, starting transfers between devices: none -> 13.3 us  [swap(): lax.ppermute(parts[m], 'group', [(i, i ^ m) for i in range(G)])]
    concatenate x5 -> x0, other arithmetic: 11.2 us -> none  [the longest x4 8.83 us: body(): jnp.concatenate([lax.dynamic_slice(partial_value, (sources[chunk, place]...]
  transfers between devices with their start and end apart: 9 -> 12, of which waited for: 8 -> 3; matrix products, arithmetic and copies ran while one was open for 9% -> 0% of each run, Pallas kernels for 6% -> 19%
where the time goes in v1:
time: 309 us
  Pallas kernels  267 us (86%)
  waiting for transfers between devices  15 us (5%)
  starting transfers between devices  13.3 us (4%)
  local copies, waits for them, and re-layouts  12.9 us (4%)
    pallas_call x1, Pallas kernels, gradient(): pl.pallas_call(functools.partial(grad_kernel, G, F, NC, LEAD, TN), out_sh...  193 us
    pallas_call x2, Pallas kernels, stats(): pl.pallas_call(functools.partial(stats_kernel, r, col_blocks), grid_spec=...  37.2 us
    pallas_call x2, Pallas kernels, condition(): pl.pallas_call(functools.partial(condition_kernel, G), grid=(N // BLK,),...  19.3 us
    ppermute x12, waiting for transfers between devices, swap(): lax.ppermute(parts[m], 'group', [(i, i ^ m) for i in range(G)])  15 us
    ppermute x12, starting transfers between devices, swap(): lax.ppermute(parts[m], 'group', [(i, i ^ m) for i in range(G)])  13.3 us
    unnamed x28, local copies, waits for them, and re-layouts  10.9 us
    pallas_call x2, Pallas kernels, relay(): pl.pallas_call(functools.partial(relay_kernel, G), grid_spec=pltpu.Prefet...  9.39 us
    pallas_call x2, Pallas kernels, place(): pl.pallas_call(functools.partial(place_kernel, G), grid=(N // BLK,), in_s...  7.67 us
  transfers between devices with their start and end apart: 12, of which 3 were waited for; matrix products, arithmetic and copies ran while one was open for 0% of the time, Pallas kernels for 19%

profile of v1, /device:TPU:0, one launch (start us, length us, event | category | flops | bytes accessed | tf_op | source)
XLA Modules:
  0.0 308.9 jit_solution(1531893764572903633)
XLA Ops:
  0.6 1.3 reshape.21.gain
  1.9 193.3 %gradient_step.1.g_ref = bf16[1024,2048]{1,0:T(8,128)(2,1)} custom-call(s32[4,4]{1,0:T(4,128)} %owners.1, bf16[1,512]{1,0:T(2,128)(2,1)} %reshape.21.gain, bf16[2048,512]{1,0:T(8,128)(2,1)} %x_hbm.1, bf16[2048,2048]{1,0:T(8,128)(2,1)} %cot_hbm.1), custom_call_target="tpu_custom_call" | custom-call | flops 34359738368 | bytes 14680064 | tf_op jit(solution)/shard_map/gradient_step/pallas_call | solution.py:274
  195.2 2.2 copy-done
  197.4 9.6 %condition_step.3 = (bf16[128,2048]{1,0:T(8,128)(2,1)S(1)}, bf16[128,2048]{1,0:T(8,128)(2,1)S(1)}, bf16[128,2048]{1,0:T(8,128)(2,1)S(1)}, bf16[128,2048]{1,0:T(8,128)(2,1)S(1)}) custom-call(bf16[1024,2048]{1,0:T(8,128)(2,1)S(1)} %copy-done, f32[1024,2048]{1,0:T(8,128)} %li_ref.7, f32[1024,2048]{1,0:T(8,128)} %ri_ref.7), custom_call_target="tpu_custom_call" | custom-call | flops 5368709120 | bytes 12582912 | tf_op jit(solution)/shard_map/condition_step/pallas_call | solution.py:372
  208.4 1.3 collective-permute-start.7
  209.8 1.5 collective-permute-start.8
  211.3 9.6 %condition_step.2 = (bf16[128,2048]{1,0:T(8,128)(2,1)S(1)}, bf16[128,2048]{1,0:T(8,128)(2,1)S(1)}, bf16[128,2048]{1,0:T(8,128)(2,1)S(1)}, bf16[128,2048]{1,0:T(8,128)(2,1)S(1)}) custom-call(bf16[1024,2048]{1,0:T(8,128)(2,1)S(1)} %copy-done, f32[1024,2048]{1,0:T(8,128)} %li_ref.7, f32[1024,2048]{1,0:T(8,128)} %ri_ref.7), custom_call_target="tpu_custom_call" | custom-call | flops 5368709120 | bytes 12582912 | tf_op jit(solution)/shard_map/condition_step/pallas_call | solution.py:372
  222.4 1.3 collective-permute-start.1
  224.5 1.5 collective-permute-start.2
  226.0 4.5 %collective-permute-done.7.refs_2_ = bf16[128,2048]{1,0:T(8,128)(2,1)} collective-permute-done((bf16[128,2048]{1,0:T(8,128)(2,1)S(1)}, bf16[128,2048]{1,0:T(8,128)(2,1)}, u32[]{:S(2)}, u32[]{:S(2)}) %collective-permute-start.7) | collective-permute-done | bytes 524320 | tf_op jit(solution)/shard_map/ppermute | solution.py:492
  230.5 3.6 %collective-permute-done.8.refs_3_ = bf16[128,2048]{1,0:T(8,128)(2,1)} collective-permute-done((bf16[128,2048]{1,0:T(8,128)(2,1)S(1)}, bf16[128,2048]{1,0:T(8,128)(2,1)}, u32[]{:S(2)}, u32[]{:S(2)}) %collective-permute-start.8) | collective-permute-done | bytes 524320 | tf_op jit(solution)/shard_map/ppermute | solution.py:492
  234.0 4.7 %relay_step.3 = (bf16[128,2048]{1,0:T(8,128)(2,1)}, bf16[128,2048]{1,0:T(8,128)(2,1)}, bf16[128,2048]{1,0:T(8,128)(2,1)}, bf16[128,2048]{1,0:T(8,128)(2,1)}) custom-call(s32[16]{0:T(128)} %reshape.20.owners, bf16[128,2048]{1,0:T(8,128)(2,1)} %copy-done.4, bf16[128,2048]{1,0:T(8,128)(2,1)} %collective-permute-done.6.refs_1_, ...), custom_call_target="tpu_custom_call" | custom-call | bytes 4194304 | tf_op jit(solution)/shard_map/relay_step/pallas_call | solution.py:454
  238.8 1.4 collective-permute-start.9
  240.1 2.2 copy-done.1
  242.3 21.2 %stats_step.2 = (f32[1024,2048]{1,0:T(8,128)}, f32[1024,2048]{1,0:T(8,128)}, f32[1024,2048]{1,0:T(8,128)}, f32[1024,2048]{1,0:T(8,128)}) custom-call(s32[8]{0:T(128)S(1)} %reshape.22.refresh, bf16[1024,2048]{1,0:T(8,128)(2,1)S(1)} %copy-done.1, f32[1024,2048]{1,0:T(8,128)} %ls_ref.3, f32[1024,2048]{1,0:T(8,128)} %rs_ref.3, f32[1024,2048]{1,0:T(8,128)} %li_ref.7, ...), custom_call_target="tpu_custom_call" | custom-call | flops 8589934592 | bytes 37748736 | tf_op jit(solution)/shard_map/stats_step/pallas_call | solution.py:417
  264.4 4.7 %relay_step.2 = (bf16[128,2048]{1,0:T(8,128)(2,1)}, bf16[128,2048]{1,0:T(8,128)(2,1)}, bf16[128,2048]{1,0:T(8,128)(2,1)}, bf16[128,2048]{1,0:T(8,128)(2,1)}) custom-call(s32[16]{0:T(128)} %reshape.20.owners, bf16[128,2048]{1,0:T(8,128)(2,1)} %copy-done.3, bf16[128,2048]{1,0:T(8,128)(2,1)} %collective-permute-done.refs_1_, ...), custom_call_target="tpu_custom_call" | custom-call | bytes 4194304 | tf_op jit(solution)/shard_map/relay_step/pallas_call | solution.py:454
  269.0 3.4 %collective-permute-start.3 = (bf16[128,2048]{1,0:T(8,128)(2,1)}, bf16[128,2048]{1,0:T(8,128)(2,1)S(1)}, u32[]{:S(2)}, u32[]{:S(2)}) collective-permute-start(bf16[128,2048]{1,0:T(8,128)(2,1)} %get-tuple-element.34), channel_id=1, source_target_pairs={{0,8},{8,0},{16,24},{24,16},{1,9},{9,1},{17,25},{25,17},{2,10},{10... | collective-permute-start | bytes 1572872 | tf_op jit(solution)/shard_map/ppermute | solution.py:492
  272.5 1.5 collective-permute-start.5
  274.0 2.2 copy-done.2
  276.2 16.0 %stats_step.3 = (f32[1024,2048]{1,0:T(8,128)}, f32[1024,2048]{1,0:T(8,128)}, f32[1024,2048]{1,0:T(8,128)}, f32[1024,2048]{1,0:T(8,128)}) custom-call(s32[8]{0:T(128)S(1)} %reshape.22.refresh, bf16[1024,2048]{1,0:T(8,128)(2,1)S(1)} %copy-done.2, f32[1024,2048]{1,0:T(8,128)} %ls_ref.3, ...), custom_call_target="tpu_custom_call", output_to_operand_aliasing={{0}: (6, {}), {1}: (7, {}), {2}: (8, {}), {3}: (9, {})} | custom-call | flops 8589934592 | bytes 37748736 | tf_op jit(solution)/shard_map/stats_step/pallas_call | solution.py:417
  293.2 3.8 %place_step.2.refs_4_ = bf16[1024,2048]{1,0:T(8,128)(2,1)} custom-call(bf16[128,2048]{1,0:T(8,128)(2,1)} %get-tuple-element.41.refs_0_, bf16[128,2048]{1,0:T(8,128)(2,1)} %copy-done.5, bf16[128,2048]{1,0:T(8,128)(2,1)} %copy-done.6, bf16[128,2048]{1,0:T(8,128)(2,1)} %copy-done.7), custom_call_target="tpu_custom_call" | custom-call | bytes 4194304 | tf_op jit(solution)/shard_map/place_step/pallas_call | solution.py:477
  297.0 7.0 %collective-permute-done.4.refs_2_ = bf16[128,2048]{1,0:T(8,128)(2,1)S(1)} collective-permute-done((bf16[128,2048]{1,0:T(8,128)(2,1)}, bf16[128,2048]{1,0:T(8,128)(2,1)S(1)}, u32[]{:S(2)}, u32[]{:S(2)}) %collective-permute-start.4) | collective-permute-done | bytes 524320 | tf_op jit(solution)/shard_map/ppermute | solution.py:492
  304.0 0.8 copy-done.10
  305.0 3.8 %place_step.3 = bf16[1024,2048]{1,0:T(8,128)(2,1)} custom-call(bf16[128,2048]{1,0:T(8,128)(2,1)} %get-tuple-element.33.refs_0_, bf16[128,2048]{1,0:T(8,128)(2,1)} %copy-done.9, bf16[128,2048]{1,0:T(8,128)(2,1)} %copy-done.10, bf16[128,2048]{1,0:T(8,128)(2,1)} %copy-done.11, bf16[1024,2048]{1,0:T(8,128)(2,1)} %place_step.2.refs_4_), custom_call_target="tpu_custom_call", output_to_operand_aliasing={{}: (4, {})} | custom-call | bytes 4194304 | tf_op jit(solution)/shard_map/place_step/pallas_call | solution.py:477
  (40 shorter events, 5.7 us)
Async XLA Ops:
  195.2 2.2 copy-start
  207.0 0.8 copy-start.4
  207.8 16.7 %collective-permute-start.6 = (bf16[128,2048]{1,0:T(8,128)(2,1)S(1)}, bf16[128,2048]{1,0:T(8,128)(2,1)}, u32[]{:S(2)}, u32[]{:S(2)}) collective-permute-start(bf16[128,2048]{1,0:T(8,128)(2,1)S(1)} %get-tuple-element.38), channel_id=1, source_target_pairs={{0,8},{8,0},{16,24},{24,16},{1,9},{9,1},{17,25},{25,17},{2,10},{10... | collective-permute-start | bytes 1572872 | tf_op jit(solution)/shard_map/ppermute | solution.py:492
  208.4 22.0 %collective-permute-start.7 = (bf16[128,2048]{1,0:T(8,128)(2,1)S(1)}, bf16[128,2048]{1,0:T(8,128)(2,1)}, u32[]{:S(2)}, u32[]{:S(2)}) collective-permute-start(bf16[128,2048]{1,0:T(8,128)(2,1)S(1)} %get-tuple-element.39), channel_id=1, source_target_pairs={{0,16},{8,24},{16,0},{24,8},{1,17},{9,25},{17,1},{25,9},{2,18},{10... | collective-permute-start | bytes 1572872 | tf_op jit(solution)/shard_map/ppermute | solution.py:492
  209.8 14.0 %copy-start.12 = (s32[4,4]{1,0:T(4,128)S(1)}, s32[4,4]{1,0:T(4,128)}, u32[]{:S(2)}) copy-start(s32[4,4]{1,0:T(4,128)} %owners.1) | copy-start | bytes 196
  209.8 14.6 %copy-start.13 = (s32[2,4]{1,0:T(2,128)S(1)}, s32[2,4]{1,0:T(2,128)}, u32[]{:S(2)}) copy-start(s32[2,4]{1,0:T(2,128)} %param.13) | copy-start | bytes 100
  209.8 24.3 %collective-permute-start.8 = (bf16[128,2048]{1,0:T(8,128)(2,1)S(1)}, bf16[128,2048]{1,0:T(8,128)(2,1)}, u32[]{:S(2)}, u32[]{:S(2)}) collective-permute-start(bf16[128,2048]{1,0:T(8,128)(2,1)S(1)} %get-tuple-element.40), channel_id=1, source_target_pairs={{0,24},{8,16},{16,8},{24,0},{1,25},{9,17},{17,9},{25,1},{2,26},{10... | collective-permute-start | bytes 1572872 | tf_op jit(solution)/shard_map/ppermute | solution.py:492
  221.8 41.7 %collective-permute-start = (bf16[128,2048]{1,0:T(8,128)(2,1)S(1)}, bf16[128,2048]{1,0:T(8,128)(2,1)}, u32[]{:S(2)}, u32[]{:S(2)}) collective-permute-start(bf16[128,2048]{1,0:T(8,128)(2,1)S(1)} %get-tuple-element.30), channel_id=1, source_target_pairs={{0,8},{8,0},{16,24},{24,16},{1,9},{9,1},{17,25},{25,17},{2,10},{10... | collective-permute-start | bytes 1572872 | tf_op jit(solution)/shard_map/ppermute | solution.py:492
  222.4 41.2 %collective-permute-start.1 = (bf16[128,2048]{1,0:T(8,128)(2,1)S(1)}, bf16[128,2048]{1,0:T(8,128)(2,1)}, u32[]{:S(2)}, u32[]{:S(2)}) collective-permute-start(bf16[128,2048]{1,0:T(8,128)(2,1)S(1)} %get-tuple-element.31), channel_id=1, source_target_pairs={{0,16},{8,24},{16,0},{24,8},{1,17},{9,25},{17,1},{25,9},{2,18},{10... | collective-permute-start | bytes 1572872 | tf_op jit(solution)/shard_map/ppermute | solution.py:492
  224.5 39.1 %collective-permute-start.2 = (bf16[128,2048]{1,0:T(8,128)(2,1)S(1)}, bf16[128,2048]{1,0:T(8,128)(2,1)S(1)}, u32[]{:S(2)}, u32[]{:S(2)}) collective-permute-start(bf16[128,2048]{1,0:T(8,128)(2,1)S(1)} %get-tuple-element.32), channel_id=1, source_target_pairs={{0,24},{8,16},{16,8},{24,0},{1,25},{9,17},{17,9},{25,1},{2,26},{10... | collective-permute-start | bytes 1572872 | tf_op jit(solution)/shard_map/ppermute | solution.py:492
  238.8 33.7 %collective-permute-start.9 = (bf16[128,2048]{1,0:T(8,128)(2,1)}, bf16[128,2048]{1,0:T(8,128)(2,1)S(1)}, u32[]{:S(2)}, u32[]{:S(2)}) collective-permute-start(bf16[128,2048]{1,0:T(8,128)(2,1)} %get-tuple-element.42), channel_id=1, source_target_pairs={{0,8},{8,0},{16,24},{24,16},{1,9},{9,1},{17,25},{25,17},{2,10},{10... | collective-permute-start | bytes 1572872 | tf_op jit(solution)/shard_map/ppermute | solution.py:492
  240.1 2.2 copy-start.1
  263.5 28.7 %collective-permute-start.10 = (bf16[128,2048]{1,0:T(8,128)(2,1)}, bf16[128,2048]{1,0:T(8,128)(2,1)S(1)}, u32[]{:S(2)}, u32[]{:S(2)}) collective-permute-start(bf16[128,2048]{1,0:T(8,128)(2,1)} %get-tuple-element.43), channel_id=1, source_target_pairs={{0,16},{8,24},{16,0},{24,8},{1,17},{9,25},{17,1},{25,9},{2,18},{10... | collective-permute-start | bytes 1572872 | tf_op jit(solution)/shard_map/ppermute | solution.py:492
  263.5 28.7 %collective-permute-start.11 = (bf16[128,2048]{1,0:T(8,128)(2,1)}, bf16[128,2048]{1,0:T(8,128)(2,1)S(1)}, u32[]{:S(2)}, u32[]{:S(2)}) collective-permute-start(bf16[128,2048]{1,0:T(8,128)(2,1)} %get-tuple-element.44), channel_id=1, source_target_pairs={{0,24},{8,16},{16,8},{24,0},{1,25},{9,17},{17,9},{25,1},{2,26},{10... | collective-permute-start | bytes 1572872 | tf_op jit(solution)/shard_map/ppermute | solution.py:492
  269.0 28.0 %collective-permute-start.3 = (bf16[128,2048]{1,0:T(8,128)(2,1)}, bf16[128,2048]{1,0:T(8,128)(2,1)S(1)}, u32[]{:S(2)}, u32[]{:S(2)}) collective-permute-start(bf16[128,2048]{1,0:T(8,128)(2,1)} %get-tuple-element.34), channel_id=1, source_target_pairs={{0,8},{8,0},{16,24},{24,16},{1,9},{9,1},{17,25},{25,17},{2,10},{10... | collective-permute-start | bytes 1572872 | tf_op jit(solution)/shard_map/ppermute | solution.py:492
  272.4 31.6 %collective-permute-start.4 = (bf16[128,2048]{1,0:T(8,128)(2,1)}, bf16[128,2048]{1,0:T(8,128)(2,1)S(1)}, u32[]{:S(2)}, u32[]{:S(2)}) collective-permute-start(bf16[128,2048]{1,0:T(8,128)(2,1)} %get-tuple-element.35), channel_id=1, source_target_pairs={{0,16},{8,24},{16,0},{24,8},{1,17},{9,25},{17,1},{25,9},{2,18},{10... | collective-permute-start | bytes 1572872 | tf_op jit(solution)/shard_map/ppermute | solution.py:492
  272.5 19.7 %copy-start.5 = (bf16[128,2048]{1,0:T(8,128)(2,1)}, bf16[128,2048]{1,0:T(8,128)(2,1)S(1)}, u32[]{:S(2)}) copy-start(bf16[128,2048]{1,0:T(8,128)(2,1)S(1)} %collective-permute-done.9.refs_1_) | copy-start | bytes 1572868
  272.5 31.5 %collective-permute-start.5 = (bf16[128,2048]{1,0:T(8,128)(2,1)}, bf16[128,2048]{1,0:T(8,128)(2,1)S(1)}, u32[]{:S(2)}, u32[]{:S(2)}) collective-permute-start(bf16[128,2048]{1,0:T(8,128)(2,1)} %get-tuple-element.36), channel_id=1, source_target_pairs={{0,24},{8,16},{16,8},{24,0},{1,25},{9,17},{17,9},{25,1},{2,26},{10... | collective-permute-start | bytes 1572872 | tf_op jit(solution)/shard_map/ppermute | solution.py:492
  274.0 2.2 copy-start.2
  292.2 0.8 copy-start.6
  292.2 0.9 copy-start.7
  297.0 7.0 %copy-start.9 = (bf16[128,2048]{1,0:T(8,128)(2,1)}, bf16[128,2048]{1,0:T(8,128)(2,1)S(1)}, u32[]{:S(2)}) copy-start(bf16[128,2048]{1,0:T(8,128)(2,1)S(1)} %collective-permute-done.3.refs_1_) | copy-start | bytes 1572868
  304.0 0.8 copy-start.10
  304.0 1.0 copy-start.11
  (2 other events, 1.6 us)

commit v2 on v1

v2 whole, which is shorter than its diff:
```python
import functools
import jax
import jax.numpy as jnp
from jax import lax
from jax.experimental import pallas as pl
from jax.experimental.pallas import tpu as pltpu
from jax.sharding import PartitionSpec as P


BLK = 512
ANY = pl.BlockSpec(memory_space=pl.ANY)
VMEM_LIMIT = 62 * 1024 * 1024
NORM_EPSILON = 1e-05
MESH = pl.DeviceIdType.MESH
RING = 8


def remote(src, dst, send_sem, recv_sem, device):
    return pltpu.make_async_remote_copy(
        src_ref=src, dst_ref=dst, send_sem=send_sem, recv_sem=recv_sem,
        device_id=device, device_id_type=MESH,
    )


def grad_kernel(G, F, NC, LAG, LEAD, owners, gain, x_hbm, cot_hbm, og, xbuf, gcol, scol, cotv, ga, ssall, res, *rest):
    nb = G.bit_length() - 1
    sends, recvs, curs = rest[:nb], rest[nb:2 * nb], rest[2 * nb:3 * nb - 1]
    lsem, ss_send, ss_recv, go, gf, gr, rs_send, rs_recv = rest[3 * nb - 1:]
    T, S = xbuf.shape
    N = cotv.shape[1]
    D = S * F
    L, q, rk, Nh = F // 2, F // G, S // NC, N // 2
    R, M = q * rk, F * rk
    W = min(BLK, Nh)
    g, f = lax.axis_index("group"), lax.axis_index("fsdp")
    l, core = f // 2, f % 2
    sib = f + 1 - 2 * core

    def bit(b):
        return (g // (1 << b)) % 2

    def partner(b):
        return g + (1 - 2 * bit(b)) * (1 << b)

    x_copy = pltpu.make_async_copy(x_hbm, xbuf, lsem.at[0])
    x_copy.start()
    cot_copy = pltpu.make_async_copy(cot_hbm, cotv, lsem.at[1])
    cot_copy.start()

    barrier = pltpu.get_barrier_semaphore()
    for d in range(1, F):
        pl.semaphore_signal(barrier, inc=1, device_id=(g, (f + d) % F), device_id_type=MESH)
    for b in range(nb):
        pl.semaphore_signal(barrier, inc=1, device_id=(partner(b), f), device_id_type=MESH)

    gcol[...] = jnp.broadcast_to(gain[...].astype(jnp.float32), (128, S)).T
    x_copy.wait()
    TT = 256
    for i in range(T // TT):
        at = slice(i * TT, (i + 1) * TT)
        v = xbuf[at, :].astype(jnp.float32).T
        ssall[f, :, at] = jnp.sum(v * v, axis=0, keepdims=True)
        v = (v * gcol[:, :1]).astype(jnp.bfloat16)
        for k in range(NC):
            ga[k, f, :, at] = v[k * rk:(k + 1) * rk]
    pl.semaphore_wait(barrier, F - 1 + nb)

    def ss_copy(slot, peer, d):
        return remote(ssall.at[slot], ssall.at[slot], ss_send.at[d - 1], ss_recv.at[slot], (g, peer))

    def piece(k, shard, send_sem, peer):
        return remote(ga.at[k, shard], ga.at[k, shard], send_sem, gr.at[k, shard], (g, peer))

    def pass_on(k, src, sems, sides, then):
        shard = 2 * src + core
        for m, side in enumerate(sides):
            for hop in (1, 2):
                peer = l + side * hop

                @pl.when((peer >= 0) & (peer <= L - 1))
                def _():
                    then(piece(k, shard, sems.at[2 * m + hop - 1], f + 2 * side * hop))

        then(piece(k, shard, sems.at[2 * len(sides)], sib))

    def own(k, then):
        pass_on(k, l, go.at[k % RING], (1, -1), then)

    def forward(k, d, then, receive):
        for side in (1, -1):
            src = l - side * d

            @pl.when((src >= 0) & (src <= L - 1))
            def _():
                if receive:
                    piece(k, 2 * src + core, go.at[0, 0], sib).wait_recv()
                pass_on(k, src, gf.at[k % 4, src], (side,) if d % 2 == 0 else (), then)

    def start(copy):
        copy.start()

    def finish(copy):
        copy.wait_send()

    def wait_sibling(k):
        for src in range(L):
            piece(k, 2 * src + 1 - core, go.at[0, 0], sib).wait_recv()

    def drain_gather(k):
        own(k, finish)
        for d in range(1, L):
            forward(k, d, finish, False)

    for d in range(1, F):
        ss_copy(f, (f + d) % F, d).start()
    own(0, start)
    own(1, start)
    for d in range(1, F):
        peer = (f + d) % F
        ss_copy(peer, peer, d).wait_recv()
    scale = lax.rsqrt(jnp.sum(ssall[...], axis=0) * (1.0 / D) + NORM_EPSILON)
    scol[...] = jnp.broadcast_to(scale, (128, T)).T
    cot_copy.wait()

    def scale_cotangent(i, _):
        rows = pl.ds(pl.multiple_of(i * 256, 256), 256)
        cotv[rows, :] = (cotv[rows, :].astype(jnp.float32) * scol[rows, :1]).astype(jnp.bfloat16)
        return 0

    def forward_all(k):
        for d in range(1, L):
            forward(k, d, start, True)

    lax.fori_loop(0, T // 256, scale_cotangent, 0)
    forward_all(0)
    for k in range(2, min(LEAD, NC)):
        own(k, start)
    ends = (l == 0) | (l == L - 1)

    def slab_at(c, place):
        found = jnp.int32(0)
        for s in range(1, G):
            found = jnp.where(owners[c, s] == place, s, found)
        return found

    def order(h):
        return list(range(nb)) if h == 0 else list(range(nb))[::-1]

    def place_of(h, i, flip, j):
        bits = order(h)
        place = jnp.int32(0)
        for m in range(i + 1):
            mine = bit(bits[m])
            place = place + (1 - mine if (flip and m == i) else mine) * (1 << bits[m])
        left = bits[i + 1:]
        for m, b in enumerate(left):
            place = place + ((j // (1 << (len(left) - 1 - m))) % 2) * (1 << b)
        return place

    def exchange(k, h, i):
        return remote(sends[i].at[k % 2, h], recvs[i].at[k, h], rs_send.at[i, k % 2, h], rs_recv.at[i, k, h],
                      (partner(order(h)[i]), f))

    def reuse(k, h, i):
        @pl.when(k >= 2)
        def _():
            exchange(k - 2, h, i).wait_send()

    def segments(h):
        for n in range(Nh // W):
            yield (h * Nh + n * W) // BLK, h * Nh + n * W, n * W

    def first_send(k, h):
        reuse(k, h, 0)
        for j in range(G // 2):
            place = place_of(h, 0, True, j)
            for c, col, at in segments(h):
                sends[0][k % 2, h, j, :, at:at + W] = res[k % (LAG + 1), slab_at(c, place), :, col:col + W]
        exchange(k, h, 0).start()

    def receive(k, i):
        for h in range(2):
            exchange(k, h, i).wait_recv()
            if i == nb - 1:
                for c, col, at in segments(h):
                    if i == 0:
                        v = res[k % (LAG + 1), slab_at(c, g), :, col:col + W].astype(jnp.float32)
                    else:
                        v = curs[i - 1][k % LAG, h, 0, :, at:at + W]
                    v = (v + recvs[i][k, h, 0, :, at:at + W].astype(jnp.float32)).astype(jnp.bfloat16)
                    for m in range(q):
                        og[pl.ds(pl.multiple_of(m * S + k * rk, rk), rk), col:col + W] = v[m * rk:(m + 1) * rk]
                continue
            reuse(k, h, i + 1)
            count = 1 << (nb - i - 2)
            mine = bit(order(h)[i + 1])
            for keep in (0, 1):
                side = mine if keep else 1 - mine
                for j in range(count):
                    at_j = side * count + j
                    place = place_of(h, i, False, at_j)
                    for c, col, at in segments(h):
                        if i == 0:
                            v = res[k % (LAG + 1), slab_at(c, place), :, col:col + W].astype(jnp.float32)
                        else:
                            v = curs[i - 1][k % LAG, h, at_j, :, at:at + W]
                        v = v + recvs[i][k, h, at_j, :, at:at + W].astype(jnp.float32)
                        if keep:
                            curs[i][k % LAG, h, j, :, at:at + W] = v
                        else:
                            sends[i + 1][k % 2, h, j, :, at:at + W] = v.astype(jnp.bfloat16)
                if not keep:
                    exchange(k, h, i + 1).start()

    def step(t, _):
        ahead = t + 1 < NC

        @pl.when(t < NC)
        def _():
            wait_sibling(t)

            @pl.when(t >= 2)
            def _():
                drain_gather(t - 2)

            @pl.when(ahead & jnp.logical_not(ends))
            def _():
                forward(t + 1, 1, start, True)

            for h in range(2):
                cols = slice(h * Nh, (h + 1) * Nh)
                v = jnp.dot(ga[t].reshape(M, T), cotv[:, cols], preferred_element_type=jnp.float32)
                res[t % (LAG + 1), :, :, cols] = v.astype(jnp.bfloat16).reshape(G, R, Nh)
                first_send(t, h)

            @pl.when(ahead & ends)
            def _():
                forward(t + 1, 1, start, True)

            @pl.when(ahead)
            def _():
                forward(t + 1, 2, start, True)

        for i in range(nb - 1, -1, -1):
            k = t - LAG * (i + 1)

            @pl.when((k >= 0) & (k < NC))
            def _():
                receive(k, i)

        @pl.when(ahead)
        def _():
            for d in range(3, L):
                forward(t + 1, d, start, True)

        @pl.when(t + LEAD < NC)
        def _():
            own(t + LEAD, start)

        return 0

    lax.fori_loop(0, NC + nb * LAG, step, 0)
    for d in range(1, F):
        ss_copy(f, (f + d) % F, d).wait_send()
    for k in range(NC - 2, NC):
        drain_gather(k)
    for i in range(nb):
        for h in range(2):
            for k in (NC - 2, NC - 1):
                exchange(k, h, i).wait_send()


def gradient(G, F, owners, gain, x, cot, NC=16, LAG=1, LEAD=3):
    NC = min(NC, x.shape[1] // 16)
    T, S = x.shape
    N = cot.shape[1]
    nb = G.bit_length() - 1
    L, q, rk, Nh = F // 2, F // G, S // NC, N // 2
    R = q * rk
    slab = S * F // G
    bf, f32 = jnp.bfloat16, jnp.float32
    counts = [G >> (i + 1) for i in range(nb)]
    dma = pltpu.SemaphoreType.DMA
    return pl.pallas_call(
        functools.partial(grad_kernel, G, F, NC, LAG, LEAD),
        out_shape=jax.ShapeDtypeStruct((slab, N), bf),
        in_specs=[
            pl.BlockSpec(memory_space=pltpu.SMEM),
            pl.BlockSpec(memory_space=pltpu.VMEM),
            pl.BlockSpec(memory_space=pl.ANY),
            pl.BlockSpec(memory_space=pl.ANY),
        ],
        out_specs=pl.BlockSpec(memory_space=pltpu.VMEM),
        scratch_shapes=[
            pltpu.VMEM((T, S), bf),
            pltpu.VMEM((S, 128), f32),
            pltpu.VMEM((T, 128), f32),
            pltpu.VMEM((T, N), bf),
            pltpu.VMEM((NC, F, rk, T), bf),
            pltpu.VMEM((F, 1, T), f32),
            pltpu.VMEM((LAG + 1, G, R, N), bf),
        ]
        + [pltpu.VMEM((2, 2, n, R, Nh), bf) for n in counts]
        + [pltpu.VMEM((NC, 2, n, R, Nh), bf) for n in counts]
        + [pltpu.VMEM((LAG, 2, n, R, Nh), f32) for n in counts[1:]]
        + [
            dma((2,)),
            dma((F - 1,)),
            dma((F,)),
            dma((RING, 5)),
            dma((4, L, 3)),
            dma((NC, F)),
            dma((nb, 2, 2)),
            dma((nb, NC, 2)),
        ],
        compiler_params=pltpu.CompilerParams(
            collective_id=0, has_side_effects=True, vmem_limit_bytes=VMEM_LIMIT
        ),
        cost_estimate=pl.CostEstimate(flops=2 * T * S * F * N, bytes_accessed=2 * (T * S + T * N + slab * N), transcendentals=0),
        name="gradient_step",
    )(owners, gain.reshape(1, S), x, cot)


SCALE_EPSILON = 1e-06
DECAY_RATE = 0.95
RIDGE_TERM = 1e-06
C0 = 1.5625
C1 = -0.3125 - 3125.0 / 4096.0
C2 = 3125.0 / 4096.0
C3 = -1250.0 / 4096.0
C4 = 250.0 / 4096.0
C5 = -25.0 / 4096.0
C6 = 1.0 / 4096.0


def dot(a, b, dims=(((1,), (0,)), ((), ()))):
    return lax.dot_general(a, b, dims, preferred_element_type=jnp.float32)


def split(value):
    high = value.astype(jnp.bfloat16)
    return high, (value - high.astype(jnp.float32)).astype(jnp.bfloat16)


def inverse_fourth_root(statistic):
    rows = lax.broadcasted_iota(jnp.int32, statistic.shape, 0)
    cols = lax.broadcasted_iota(jnp.int32, statistic.shape, 1)
    diagonal = rows == cols
    matrix = statistic + jnp.where(diagonal, RIDGE_TERM, 0.0)
    scaling = 2.5 * lax.rsqrt(jnp.sum(matrix * matrix, keepdims=True))
    m1 = scaling * matrix
    m1_low = m1.astype(jnp.bfloat16)
    m2 = dot(m1_low, m1_low)
    m3 = dot(m2.astype(jnp.bfloat16), m1_low)
    upper = dot(
        m3.astype(jnp.bfloat16), (C4 * m1 + C5 * m2 + C6 * m3).astype(jnp.bfloat16)
    )
    total = C1 * m1 + C2 * m2 + C3 * m3 + upper + jnp.where(diagonal, C0, 0.0)
    return jnp.sqrt(jnp.sqrt(scaling)) * total


def condition_kernel(G, g_ref, li_ref, ri_ref, *rest):
    outs, held = rest[-G - 1:-1], rest[-1]
    me = lax.axis_index("group")
    grad = g_ref[...]
    left_high, left_low = split(li_ref[...])
    half = dot(left_high, grad) + dot(left_low, grad)
    half_high, half_low = split(half)
    right_high, right_low = split(ri_ref[...])
    conditioned = dot(half_high, right_high) + dot(half_low, right_high) + dot(half_high, right_low)
    mean = jnp.sum(conditioned * conditioned, keepdims=True) * (1.0 / conditioned.size)
    held[...] = (conditioned * lax.rsqrt(mean + SCALE_EPSILON)).astype(jnp.bfloat16)
    rows = BLK // G
    for m in range(G):
        outs[m][...] = held[pl.ds(pl.multiple_of((me ^ m) * rows, rows), rows), :]


def condition(G, unit, grad, left, right, after):
    r, first, count = unit
    N = count * BLK
    here = pl.BlockSpec((BLK, BLK), lambda c: (r, first + c))
    part = pl.BlockSpec((BLK // G, BLK), lambda c: (0, c))
    return pl.pallas_call(
        functools.partial(condition_kernel, G),
        grid=(N // BLK,),
        in_specs=[here] * 3 + [ANY] * len(after),
        out_specs=[part] * G,
        out_shape=[jax.ShapeDtypeStruct((BLK // G, N), jnp.bfloat16)] * G,
        scratch_shapes=[pltpu.VMEM((BLK, BLK), jnp.bfloat16)],
        compiler_params=pltpu.CompilerParams(
            dimension_semantics=("arbitrary",), vmem_limit_bytes=VMEM_LIMIT
        ),
        cost_estimate=pl.CostEstimate(
            flops=(N // BLK) * 5 * 2 * BLK**3, bytes_accessed=(N // BLK) * 12 * BLK * BLK, transcendentals=0
        ),
        name="condition_step",
    )(grad, left, right, *after)


def stats_kernel(r, col_blocks, refresh, g_ref, ls_ref, rs_ref, li_ref, ri_ref, *rest):
    la_ref, ra_ref, ln_ref, rn_ref, token = rest[-5:]
    token[...] = jnp.zeros_like(token)
    grad = g_ref[...]
    la_ref[...] = DECAY_RATE * ls_ref[...] + (1.0 - DECAY_RATE) * dot(
        grad, grad, (((1,), (1,)), ((), ()))
    )
    ra_ref[...] = DECAY_RATE * rs_ref[...] + (1.0 - DECAY_RATE) * dot(
        grad, grad, (((0,), (0,)), ((), ()))
    )
    flag = refresh[r * col_blocks + pl.program_id(0)]

    @pl.when(flag > 0)
    def _():
        ln_ref[...] = inverse_fourth_root(la_ref[...])
        rn_ref[...] = inverse_fourth_root(ra_ref[...])

    @pl.when(flag <= 0)
    def _():
        ln_ref[...] = li_ref[...]
        rn_ref[...] = ri_ref[...]


def stats(r, grad, refresh, states, previous, after):
    slab_rows, N = states[0].shape
    col_blocks = N // BLK
    here = pl.BlockSpec((BLK, BLK), lambda c, flags: (r, c))
    held = [ANY] * (len(previous) + len(after))
    whole = jax.ShapeDtypeStruct((slab_rows, N), jnp.float32)
    return pl.pallas_call(
        functools.partial(stats_kernel, r, col_blocks),
        grid_spec=pltpu.PrefetchScalarGridSpec(
            num_scalar_prefetch=1,
            grid=(col_blocks,),
            in_specs=[here] * 5 + held,
            out_specs=[here] * 4 + [pl.BlockSpec((8, 128), lambda c, flags: (0, 0))],
        ),
        out_shape=[whole] * 4 + [jax.ShapeDtypeStruct((8, 128), jnp.float32)],
        input_output_aliases={6 + i: i for i in range(len(previous))},
        compiler_params=pltpu.CompilerParams(
            dimension_semantics=("arbitrary",), vmem_limit_bytes=VMEM_LIMIT
        ),
        cost_estimate=pl.CostEstimate(
            flops=col_blocks * 8 * 2 * BLK**3,
            bytes_accessed=col_blocks * 9 * 4 * BLK * BLK,
            transcendentals=0,
        ),
        name="stats_step",
    )(refresh, grad, *states, *previous, *after)


def relay_kernel(G, first, owners, *refs):
    ins, outs = refs[:G], refs[-G:]
    me = lax.axis_index("group")
    c = first + pl.program_id(0)
    for m in range(G):
        wanted = owners[c * G + (me ^ m)] ^ me
        for k in range(G):
            @pl.when(wanted == k)
            def _():
                outs[m][...] = ins[k][...]


def relay(G, unit, owners, parts, after):
    rows, N = parts[0].shape
    part = pl.BlockSpec((rows, BLK), lambda c, own: (0, c))
    return pl.pallas_call(
        functools.partial(relay_kernel, G, unit[1]),
        grid_spec=pltpu.PrefetchScalarGridSpec(
            num_scalar_prefetch=1, grid=(N // BLK,), in_specs=[part] * G + [ANY] * len(after), out_specs=[part] * G
        ),
        out_shape=[jax.ShapeDtypeStruct((rows, N), jnp.bfloat16)] * G,
        compiler_params=pltpu.CompilerParams(
            dimension_semantics=("arbitrary",), vmem_limit_bytes=VMEM_LIMIT
        ),
        cost_estimate=pl.CostEstimate(flops=0, bytes_accessed=4 * G * rows * N, transcendentals=0),
        name="relay_step",
    )(owners, *parts, *after)


def place_kernel(G, *refs):
    ins, out = refs[:G], refs[-1]
    me = lax.axis_index("group")
    rows = BLK // G
    for m in range(G):
        out[pl.ds(pl.multiple_of((me ^ m) * rows, rows), rows), :] = ins[m][...]


def place(G, unit, shape, parts, previous, after):
    rows, N = parts[0].shape
    r, first = unit[:2]
    part = pl.BlockSpec((rows, BLK), lambda c: (0, c))
    return pl.pallas_call(
        functools.partial(place_kernel, G),
        grid=(N // BLK,),
        in_specs=[part] * G + [ANY] * (len(previous) + len(after)),
        out_specs=pl.BlockSpec((BLK, BLK), lambda c: (r, first + c)),
        out_shape=jax.ShapeDtypeStruct(shape, jnp.bfloat16),
        input_output_aliases={G: 0} if previous else {},
        compiler_params=pltpu.CompilerParams(
            dimension_semantics=("arbitrary",), vmem_limit_bytes=VMEM_LIMIT
        ),
        cost_estimate=pl.CostEstimate(flops=0, bytes_accessed=4 * BLK * N, transcendentals=0),
        name="place_step",
    )(*parts, *previous, *after)


def swap(G, parts):
    out = [parts[0]]
    for m in range(1, G):
        out.append(lax.ppermute(parts[m], "group", [(i, i ^ m) for i in range(G)]))
    return out


def cut(count, blocks):
    units = []
    for r in range(count):
        cuts = [0, 1, blocks] if r == 0 and blocks > 1 else [0, blocks]
        units += [(r, lo, hi - lo) for lo, hi in zip(cuts, cuts[1:])]
    return units


def body(G, F, inputs, norm_gain, cotangent, owners, refresh, *states):
    slab_rows, N = states[0].shape
    own = gradient(G, F, owners, norm_gain, inputs, cotangent)
    flat_owners = owners.reshape(-1)
    count, blocks = slab_rows // BLK, N // BLK
    units = cut(count, blocks)
    sent, back, after = [], [], ()
    for unit in units:
        parts = condition(G, unit, own, states[2], states[3], after)
        after = (parts[0],)
        sent.append(swap(G, parts))
    previous = ()
    for r in range(count):
        *previous, token = stats(r, own, refresh.reshape(-1), states, tuple(previous), after)
        after = (token,)
        if r == 0:
            for unit, parts in zip(units, sent):
                parts = relay(G, unit, flat_owners, parts, after)
                after = (parts[0],)
                back.append(swap(G, parts))
    update = ()
    for unit, parts in zip(units, back):
        update = (place(G, unit, (slab_rows, N), parts, update, after),)
    return (*update, *previous)


def solution(mesh):
    spec = P("group", "fsdp")
    in_specs = (spec, P("fsdp"), spec, P("fsdp", None), spec, spec, spec, spec, spec)
    G, F = mesh.shape["group"], mesh.shape["fsdp"]

    def whole(*args):
        def local(*blocks_of):
            return body(G, F, *blocks_of)

        step = jax.shard_map(
            local, mesh=mesh, in_specs=in_specs, out_specs=(spec,) * 5, check_vma=False
        )
        return step(*args)

    return whole
```

time: 309 us -> 305 us (0.987)
  Pallas kernels: 267 us -> 252 us
  waiting for transfers between devices: 15 us -> 25.3 us
  starting transfers between devices: 13.3 us -> 20.8 us
  local copies, waits for them, and re-layouts: 12.9 us -> 5.47 us
    pallas_call x3 -> x4, Pallas kernels: 203 us -> 187 us  [the longest x1 175 us: gradient(): pl.pallas_call(functools.partial(grad_kernel, G, F, NC, LAG, LEAD), out_s...]
    ppermute x12 -> x18, waiting for transfers between devices: 15 us -> 25.3 us  [swap(): out.append(lax.ppermute(parts[m], 'group', [(i, i ^ m) for i in range(G)]))]
    unnamed x28, local copies, waits for them, and re-layouts: 10.9 us -> 2.92 us
    ppermute x12 -> x18, starting transfers between devices: 13.3 us -> 20.8 us  [swap(): out.append(lax.ppermute(parts[m], 'group', [(i, i ^ m) for i in range(G)]))]
    pallas_call x2, Pallas kernels: 37.2 us -> 32.9 us  [stats(): pl.pallas_call(functools.partial(stats_kernel, r, col_blocks), grid_spec=...]
    pallas_call x2 -> x3, Pallas kernels: 19.3 us -> 23.2 us  [condition(): pl.pallas_call(functools.partial(condition_kernel, G), grid=(N // BLK,),...]
    pallas_call x2 -> x3, Pallas kernels: 7.67 us -> 9.22 us  [place(): pl.pallas_call(functools.partial(place_kernel, G), grid=(N // BLK,), in_s...]
  transfers between devices with their start and end apart: 12 -> 18, of which waited for: 3 -> 4; matrix products, arithmetic and copies ran while one was open for 0% -> 0% of each run, Pallas kernels for 19% -> 20%
where the time goes in v2:
time: 305 us; the launch traced here: 304 us
  Pallas kernels  252 us (83%)
  waiting for transfers between devices  25.3 us (8%)
  starting transfers between devices  20.8 us (7%)
  local copies, waits for them, and re-layouts  5.47 us (2%)
    pallas_call x1, Pallas kernels, gradient(): pl.pallas_call(functools.partial(grad_kernel, G, F, NC, LAG, LEAD), out_s...  175 us
    pallas_call x2, Pallas kernels, stats(): pl.pallas_call(functools.partial(stats_kernel, r, col_blocks), grid_spec=...  32.9 us
    ppermute x18, waiting for transfers between devices, swap(): out.append(lax.ppermute(parts[m], 'group', [(i, i ^ m) for i in range(G)]))  25.3 us
    pallas_call x3, Pallas kernels, condition(): pl.pallas_call(functools.partial(condition_kernel, G), grid=(N // BLK,),...  23.2 us
    ppermute x18, starting transfers between devices, swap(): out.append(lax.ppermute(parts[m], 'group', [(i, i ^ m) for i in range(G)]))  20.8 us
    pallas_call x3, Pallas kernels, relay(): pl.pallas_call(functools.partial(relay_kernel, G, unit[1]), grid_spec=plt...  11.8 us
    pallas_call x3, Pallas kernels, place(): pl.pallas_call(functools.partial(place_kernel, G), grid=(N // BLK,), in_s...  9.22 us
  transfers between devices with their start and end apart: 18, of which 4 were waited for; matrix products, arithmetic and copies ran while one was open for 0% of the time, Pallas kernels for 20%

profile of v2, /device:TPU:0, one launch (start us, length us, event | category | flops | bytes accessed | tf_op | source)
XLA Modules:
  0.0 304.5 jit_solution(18243357558389520986)
XLA Ops:
  1.9 175.1 %gradient_step.1.g_ref = bf16[1024,2048]{1,0:T(8,128)(2,1)} custom-call(s32[4,4]{1,0:T(4,128)} %owners.1, bf16[1,512]{1,0:T(2,128)(2,1)} %reshape.21.gain, bf16[2048,512]{1,0:T(8,128)(2,1)} %x_hbm.1, bf16[2048,2048]{1,0:T(8,128)(2,1)} %cot_hbm.1), custom_call_target="tpu_custom_call" | custom-call | flops 34359738368 | bytes 14680064 | tf_op jit(solution)/shard_map/gradient_step/pallas_call | solution.py:284
  177.0 4.4 %condition_step.3 = (bf16[128,512]{1,0:T(8,128)(2,1)}, bf16[128,512]{1,0:T(8,128)(2,1)}, bf16[128,512]{1,0:T(8,128)(2,1)}, bf16[128,512]{1,0:T(8,128)(2,1)}) custom-call(bf16[1024,2048]{1,0:T(8,128)(2,1)} %gradient_step.1.g_ref, f32[1024,2048]{1,0:T(8,128)} %li_ref.9, f32[1024,2048]{1,0:T(8,128)} %ri_ref.9), custom_call_target="tpu_custom_call" | custom-call | flops 1342177280 | bytes 3145728 | tf_op jit(solution)/shard_map/condition_step/pallas_call | solution.py:383
  181.4 8.4 %condition_step.4 = (bf16[128,1536]{1,0:T(8,128)(2,1)}, bf16[128,1536]{1,0:T(8,128)(2,1)}, bf16[128,1536]{1,0:T(8,128)(2,1)}, bf16[128,1536]{1,0:T(8,128)(2,1)}) custom-call(bf16[1024,2048]{1,0:T(8,128)(2,1)} %gradient_step.1.g_ref, f32[1024,2048]{1,0:T(8,128)} %li_ref.9, f32[1024,2048]{1,0:T(8,128)} %ri_ref.9, ...), custom_call_target="tpu_custom_call" | custom-call | flops 4026531840 | bytes 9437184 | tf_op jit(solution)/shard_map/condition_step/pallas_call | solution.py:383
  190.4 1.4 collective-permute-start.6
  192.5 1.4 collective-permute-start.8
  193.9 10.4 %condition_step.5 = (bf16[128,2048]{1,0:T(8,128)(2,1)}, bf16[128,2048]{1,0:T(8,128)(2,1)}, bf16[128,2048]{1,0:T(8,128)(2,1)}, bf16[128,2048]{1,0:T(8,128)(2,1)}) custom-call(bf16[1024,2048]{1,0:T(8,128)(2,1)} %gradient_step.1.g_ref, f32[1024,2048]{1,0:T(8,128)} %li_ref.9, f32[1024,2048]{1,0:T(8,128)} %ri_ref.9, ...), custom_call_target="tpu_custom_call" | custom-call | flops 5368709120 | bytes 12582912 | tf_op jit(solution)/shard_map/condition_step/pallas_call | solution.py:383
  204.3 1.4 collective-permute-start
  208.3 1.4 collective-permute-start.2
  209.7 1.3 collective-permute-start.4
  211.1 1.5 collective-permute-start.5
  212.6 16.5 %stats_step.2 = (f32[1024,2048]{1,0:T(8,128)}, f32[1024,2048]{1,0:T(8,128)}, f32[1024,2048]{1,0:T(8,128)}, f32[1024,2048]{1,0:T(8,128)}, f32[8,128]{1,0:T(8,128)}) custom-call(s32[8]{0:T(128)} %reshape.22.refresh, bf16[1024,2048]{1,0:T(8,128)(2,1)} %gradient_step.1.g_ref, f32[1024,2048]{1,0:T(8,128)} %ls_ref.3, f32[1024,2048]{1,0:T(8,128)} %rs_ref.3, ...), custom_call_target="tpu_custom_call" | custom-call | flops 8589934592 | bytes 37748736 | tf_op jit(solution)/shard_map/stats_step/pallas_call | solution.py:429
  229.7 2.7 relay_step.3
  232.4 15.1 %collective-permute-done.4.refs_2_ = bf16[128,1536]{1,0:T(8,128)(2,1)} collective-permute-done((bf16[128,1536]{1,0:T(8,128)(2,1)}, bf16[128,1536]{1,0:T(8,128)(2,1)}, u32[]{:S(2)}, u32[]{:S(2)}) %collective-permute-start.4) | collective-permute-done | bytes 393248 | tf_op jit(solution)/shard_map/ppermute | solution.py:510
  247.5 4.5 %relay_step.4 = (bf16[128,1536]{1,0:T(8,128)(2,1)}, bf16[128,1536]{1,0:T(8,128)(2,1)}, bf16[128,1536]{1,0:T(8,128)(2,1)}, bf16[128,1536]{1,0:T(8,128)(2,1)}) custom-call(s32[16]{0:T(128)} %reshape.20.owners, bf16[128,1536]{1,0:T(8,128)(2,1)} %get-tuple-element.40.rest_0_.refs_0_, bf16[128,1536]{1,0:T(8,128)(2,1)} %copy-done.7, ...), custom_call_target="tpu_custom_call" | custom-call | bytes 3145728 | tf_op jit(solution)/shard_map/relay_step/pallas_call | solution.py:466
  254.8 1.4 collective-permute-start.17
  257.5 4.7 %relay_step.5 = (bf16[128,2048]{1,0:T(8,128)(2,1)}, bf16[128,2048]{1,0:T(8,128)(2,1)}, bf16[128,2048]{1,0:T(8,128)(2,1)}, bf16[128,2048]{1,0:T(8,128)(2,1)}) custom-call(s32[16]{0:T(128)} %reshape.20.owners, bf16[128,2048]{1,0:T(8,128)(2,1)} %get-tuple-element.41.rest_0_.refs_0_, bf16[128,2048]{1,0:T(8,128)(2,1)} %copy-done.3, bf16[128,2048]{1,0:T(8,128)(2,1)} %copy-done.4, ...), custom_call_target="tpu_custom_call" | custom-call | bytes 4194304 | tf_op jit(solution)/shard_map/relay_step/pallas_call | solution.py:466
  262.2 4.3 %collective-permute-done.15.refs_1_ = bf16[128,512]{1,0:T(8,128)(2,1)} collective-permute-done((bf16[128,512]{1,0:T(8,128)(2,1)}, bf16[128,512]{1,0:T(8,128)(2,1)}, u32[]{:S(2)}, u32[]{:S(2)}) %collective-permute-start.15) | collective-permute-done | bytes 131104 | tf_op jit(solution)/shard_map/ppermute | solution.py:510
  266.4 1.4 collective-permute-start.14
  270.8 1.4 collective-permute-start.11
  272.2 16.4 %stats_step.3 = (f32[1024,2048]{1,0:T(8,128)}, f32[1024,2048]{1,0:T(8,128)}, f32[1024,2048]{1,0:T(8,128)}, f32[1024,2048]{1,0:T(8,128)}, f32[8,128]{1,0:T(8,128)}) custom-call(s32[8]{0:T(128)} %reshape.22.refresh, bf16[1024,2048]{1,0:T(8,128)(2,1)} %gradient_step.1.g_ref, ...), custom_call_target="tpu_custom_call", output_to_operand_aliasing={{0}: (6, {}), {1}: (7, {}), {2}: (8, {}), {3}: (9, {})} | custom-call | flops 8589934592 | bytes 37748736 | tf_op jit(solution)/shard_map/stats_step/pallas_call | solution.py:429
  288.7 1.9 place_step.3.refs_4_
  290.6 3.5 %place_step.4.refs_4_ = bf16[1024,2048]{1,0:T(8,128)(2,1)} custom-call(bf16[128,1536]{1,0:T(8,128)(2,1)} %get-tuple-element.53.refs_4_.refs_0_, bf16[128,1536]{1,0:T(8,128)(2,1)} %copy-done.6, bf16[128,1536]{1,0:T(8,128)(2,1)} %collective-permute-done.13.refs_2_, bf16[128,1536]{1,0:T(8,128)(2,1)} %collective-permute-done.14.refs_3_, ...), custom_call_target="tpu_custom_call", output_to_operand_aliasing={{}: (4, {})} | custom-call | bytes 3145728 | tf_op jit(solution)/shard_map/place_step/pallas_call | solution.py:492
  294.1 5.0 %collective-permute-done.10.refs_2_ = bf16[128,2048]{1,0:T(8,128)(2,1)S(1)} collective-permute-done((bf16[128,2048]{1,0:T(8,128)(2,1)}, bf16[128,2048]{1,0:T(8,128)(2,1)S(1)}, u32[]{:S(2)}, u32[]{:S(2)}) %collective-permute-start.10) | collective-permute-done | bytes 524320 | tf_op jit(solution)/shard_map/ppermute | solution.py:510
  300.6 3.8 %place_step.5 = bf16[1024,2048]{1,0:T(8,128)(2,1)} custom-call(bf16[128,2048]{1,0:T(8,128)(2,1)} %get-tuple-element.54.rest_4_.refs_0_, bf16[128,2048]{1,0:T(8,128)(2,1)} %copy-done, bf16[128,2048]{1,0:T(8,128)(2,1)} %copy-done.1, bf16[128,2048]{1,0:T(8,128)(2,1)} %copy-done.2, ...), custom_call_target="tpu_custom_call", output_to_operand_aliasing={{}: (4, {})} | custom-call | bytes 4194304 | tf_op jit(solution)/shard_map/place_step/pallas_call | solution.py:492
  (55 shorter events, 14.5 us)
Async XLA Ops:
  181.4 9.1 %copy-start.12 = (bf16[128,512]{1,0:T(8,128)(2,1)S(1)}, bf16[128,512]{1,0:T(8,128)(2,1)}, u32[]{:S(2)}) copy-start(bf16[128,512]{1,0:T(8,128)(2,1)} %get-tuple-element.48) | copy-start | bytes 393220
  181.4 10.5 %copy-start.11 = (bf16[128,512]{1,0:T(8,128)(2,1)S(1)}, bf16[128,512]{1,0:T(8,128)(2,1)}, u32[]{:S(2)}) copy-start(bf16[128,512]{1,0:T(8,128)(2,1)} %get-tuple-element.49) | copy-start | bytes 393220
  189.8 21.3 %collective-permute-start.3 = (bf16[128,1536]{1,0:T(8,128)(2,1)}, bf16[128,1536]{1,0:T(8,128)(2,1)S(1)}, u32[]{:S(2)}, u32[]{:S(2)}) collective-permute-start(bf16[128,1536]{1,0:T(8,128)(2,1)} %get-tuple-element.45), channel_id=1, source_target_pairs={{0,8},{8,0},{16,24},{24,16},{1,9},{9,1},{17,25},{25,17},{2,10},{10... | collective-permute-start | bytes 1179656 | tf_op jit(solution)/shard_map/ppermute | solution.py:510
  190.4 15.9 %collective-permute-start.6 = (bf16[128,512]{1,0:T(8,128)(2,1)S(1)}, bf16[128,512]{1,0:T(8,128)(2,1)S(1)}, u32[]{:S(2)}, u32[]{:S(2)}) collective-permute-start(bf16[128,512]{1,0:T(8,128)(2,1)S(1)} %copy-done.12), channel_id=1, source_target_pairs={{0,8},{8,0},{16,24},{24,16},{1,9},{9,1},{17,25},{25,17},{2,10},{10... | collective-permute-start | bytes 393224 | tf_op jit(solution)/shard_map/ppermute | solution.py:510
  191.8 15.8 %collective-permute-start.7 = (bf16[128,512]{1,0:T(8,128)(2,1)S(1)}, bf16[128,512]{1,0:T(8,128)(2,1)S(1)}, u32[]{:S(2)}, u32[]{:S(2)}) collective-permute-start(bf16[128,512]{1,0:T(8,128)(2,1)S(1)} %copy-done.11), channel_id=1, source_target_pairs={{0,16},{8,24},{16,0},{24,8},{1,17},{9,25},{17,1},{25,9},{2,18},{10... | collective-permute-start | bytes 393224 | tf_op jit(solution)/shard_map/ppermute | solution.py:510
  192.5 17.3 %collective-permute-start.8 = (bf16[128,512]{1,0:T(8,128)(2,1)}, bf16[128,512]{1,0:T(8,128)(2,1)}, u32[]{:S(2)}, u32[]{:S(2)}) collective-permute-start(bf16[128,512]{1,0:T(8,128)(2,1)} %get-tuple-element.50), channel_id=1, source_target_pairs={{0,24},{8,16},{16,8},{24,0},{1,25},{9,17},{17,9},{25,1},{2,26},{10... | collective-permute-start | bytes 393224 | tf_op jit(solution)/shard_map/ppermute | solution.py:510
  193.9 11.7 %copy-start.13 = (s32[2,4]{1,0:T(2,128)S(1)}, s32[2,4]{1,0:T(2,128)}, u32[]{:S(2)}) copy-start(s32[2,4]{1,0:T(2,128)} %param.13) | copy-start | bytes 100
  204.3 49.8 %collective-permute-start = (bf16[128,2048]{1,0:T(8,128)(2,1)}, bf16[128,2048]{1,0:T(8,128)(2,1)S(1)}, u32[]{:S(2)}, u32[]{:S(2)}) collective-permute-start(bf16[128,2048]{1,0:T(8,128)(2,1)} %get-tuple-element.42), channel_id=1, source_target_pairs={{0,8},{8,0},{16,24},{24,16},{1,9},{9,1},{17,25},{25,17},{2,10},{10... | collective-permute-start | bytes 1572872 | tf_op jit(solution)/shard_map/ppermute | solution.py:510
  207.0 47.9 %collective-permute-start.1 = (bf16[128,2048]{1,0:T(8,128)(2,1)}, bf16[128,2048]{1,0:T(8,128)(2,1)S(1)}, u32[]{:S(2)}, u32[]{:S(2)}) collective-permute-start(bf16[128,2048]{1,0:T(8,128)(2,1)} %get-tuple-element.43), channel_id=1, source_target_pairs={{0,16},{8,24},{16,0},{24,8},{1,17},{9,25},{17,1},{25,9},{2,18},{10... | collective-permute-start | bytes 1572872 | tf_op jit(solution)/shard_map/ppermute | solution.py:510
  208.3 48.0 %collective-permute-start.2 = (bf16[128,2048]{1,0:T(8,128)(2,1)}, bf16[128,2048]{1,0:T(8,128)(2,1)S(1)}, u32[]{:S(2)}, u32[]{:S(2)}) collective-permute-start(bf16[128,2048]{1,0:T(8,128)(2,1)} %get-tuple-element.44), channel_id=1, source_target_pairs={{0,24},{8,16},{16,8},{24,0},{1,25},{9,17},{17,9},{25,1},{2,26},{10... | collective-permute-start | bytes 1572872 | tf_op jit(solution)/shard_map/ppermute | solution.py:510
  209.7 37.8 %collective-permute-start.4 = (bf16[128,1536]{1,0:T(8,128)(2,1)}, bf16[128,1536]{1,0:T(8,128)(2,1)}, u32[]{:S(2)}, u32[]{:S(2)}) collective-permute-start(bf16[128,1536]{1,0:T(8,128)(2,1)} %get-tuple-element.46), channel_id=1, source_target_pairs={{0,16},{8,24},{16,0},{24,8},{1,17},{9,25},{17,1},{25,9},{2,18},{10... | collective-permute-start | bytes 1179656 | tf_op jit(solution)/shard_map/ppermute | solution.py:510
  211.1 18.0 %copy-start.7 = (bf16[128,1536]{1,0:T(8,128)(2,1)}, bf16[128,1536]{1,0:T(8,128)(2,1)S(1)}, u32[]{:S(2)}) copy-start(bf16[128,1536]{1,0:T(8,128)(2,1)S(1)} %collective-permute-done.3.refs_1_) | copy-start | bytes 1179652
  211.1 36.5 %collective-permute-start.5 = (bf16[128,1536]{1,0:T(8,128)(2,1)}, bf16[128,1536]{1,0:T(8,128)(2,1)}, u32[]{:S(2)}, u32[]{:S(2)}) collective-permute-start(bf16[128,1536]{1,0:T(8,128)(2,1)} %get-tuple-element.47), channel_id=1, source_target_pairs={{0,24},{8,16},{16,8},{24,0},{1,25},{9,17},{17,9},{25,1},{2,26},{10... | collective-permute-start | bytes 1179656 | tf_op jit(solution)/shard_map/ppermute | solution.py:510
  212.6 16.5 %copy-start.10 = (s32[4,4]{1,0:T(4,128)S(1)}, s32[4,4]{1,0:T(4,128)}, u32[]{:S(2)}) copy-start(s32[4,4]{1,0:T(4,128)} %owners.1) | copy-start | bytes 196
  252.0 18.8 %collective-permute-start.12 = (bf16[128,1536]{1,0:T(8,128)(2,1)}, bf16[128,1536]{1,0:T(8,128)(2,1)S(1)}, u32[]{:S(2)}, u32[]{:S(2)}) collective-permute-start(bf16[128,1536]{1,0:T(8,128)(2,1)} %get-tuple-element.58), channel_id=1, source_target_pairs={{0,8},{8,0},{16,24},{24,16},{1,9},{9,1},{17,25},{25,17},{2,10},{10... | collective-permute-start | bytes 1179656 | tf_op jit(solution)/shard_map/ppermute | solution.py:510
  252.7 13.7 %collective-permute-start.15 = (bf16[128,512]{1,0:T(8,128)(2,1)}, bf16[128,512]{1,0:T(8,128)(2,1)}, u32[]{:S(2)}, u32[]{:S(2)}) collective-permute-start(bf16[128,512]{1,0:T(8,128)(2,1)} %get-tuple-element.61), channel_id=1, source_target_pairs={{0,8},{8,0},{16,24},{24,16},{1,9},{9,1},{17,25},{25,17},{2,10},{10... | collective-permute-start | bytes 393224 | tf_op jit(solution)/shard_map/ppermute | solution.py:510
  254.0 13.8 %collective-permute-start.16 = (bf16[128,512]{1,0:T(8,128)(2,1)}, bf16[128,512]{1,0:T(8,128)(2,1)}, u32[]{:S(2)}, u32[]{:S(2)}) collective-permute-start(bf16[128,512]{1,0:T(8,128)(2,1)} %get-tuple-element.62), channel_id=1, source_target_pairs={{0,16},{8,24},{16,0},{24,8},{1,17},{9,25},{17,1},{25,9},{2,18},{10... | collective-permute-start | bytes 393224 | tf_op jit(solution)/shard_map/ppermute | solution.py:510
  254.8 14.8 %collective-permute-start.17 = (bf16[128,512]{1,0:T(8,128)(2,1)}, bf16[128,512]{1,0:T(8,128)(2,1)}, u32[]{:S(2)}, u32[]{:S(2)}) collective-permute-start(bf16[128,512]{1,0:T(8,128)(2,1)} %get-tuple-element.63), channel_id=1, source_target_pairs={{0,24},{8,16},{16,8},{24,0},{1,25},{9,17},{17,9},{25,1},{2,26},{10... | collective-permute-start | bytes 393224 | tf_op jit(solution)/shard_map/ppermute | solution.py:510
  256.3 34.3 %collective-permute-start.13 = (bf16[128,1536]{1,0:T(8,128)(2,1)}, bf16[128,1536]{1,0:T(8,128)(2,1)}, u32[]{:S(2)}, u32[]{:S(2)}) collective-permute-start(bf16[128,1536]{1,0:T(8,128)(2,1)} %get-tuple-element.59), channel_id=1, source_target_pairs={{0,16},{8,24},{16,0},{24,8},{1,17},{9,25},{17,1},{25,9},{2,18},{10... | collective-permute-start | bytes 1179656 | tf_op jit(solution)/shard_map/ppermute | solution.py:510
  266.4 24.2 %collective-permute-start.14 = (bf16[128,1536]{1,0:T(8,128)(2,1)}, bf16[128,1536]{1,0:T(8,128)(2,1)}, u32[]{:S(2)}, u32[]{:S(2)}) collective-permute-start(bf16[128,1536]{1,0:T(8,128)(2,1)} %get-tuple-element.60), channel_id=1, source_target_pairs={{0,24},{8,16},{16,8},{24,0},{1,25},{9,17},{17,9},{25,1},{2,26},{10... | collective-permute-start | bytes 1179656 | tf_op jit(solution)/shard_map/ppermute | solution.py:510
  267.9 26.2 %collective-permute-start.9 = (bf16[128,2048]{1,0:T(8,128)(2,1)}, bf16[128,2048]{1,0:T(8,128)(2,1)S(1)}, u32[]{:S(2)}, u32[]{:S(2)}) collective-permute-start(bf16[128,2048]{1,0:T(8,128)(2,1)} %get-tuple-element.55), channel_id=1, source_target_pairs={{0,8},{8,0},{16,24},{24,16},{1,9},{9,1},{17,25},{25,17},{2,10},{10... | collective-permute-start | bytes 1572872 | tf_op jit(solution)/shard_map/ppermute | solution.py:510
  269.6 29.4 %collective-permute-start.10 = (bf16[128,2048]{1,0:T(8,128)(2,1)}, bf16[128,2048]{1,0:T(8,128)(2,1)S(1)}, u32[]{:S(2)}, u32[]{:S(2)}) collective-permute-start(bf16[128,2048]{1,0:T(8,128)(2,1)} %get-tuple-element.56), channel_id=1, source_target_pairs={{0,16},{8,24},{16,0},{24,8},{1,17},{9,25},{17,1},{25,9},{2,18},{10... | collective-permute-start | bytes 1572872 | tf_op jit(solution)/shard_map/ppermute | solution.py:510
  270.8 17.8 %copy-start.6 = (bf16[128,1536]{1,0:T(8,128)(2,1)}, bf16[128,1536]{1,0:T(8,128)(2,1)S(1)}, u32[]{:S(2)}) copy-start(bf16[128,1536]{1,0:T(8,128)(2,1)S(1)} %collective-permute-done.12.refs_1_) | copy-start | bytes 1179652
  270.8 28.2 %collective-permute-start.11 = (bf16[128,2048]{1,0:T(8,128)(2,1)}, bf16[128,2048]{1,0:T(8,128)(2,1)S(1)}, u32[]{:S(2)}, u32[]{:S(2)}) collective-permute-start(bf16[128,2048]{1,0:T(8,128)(2,1)} %get-tuple-element.57), channel_id=1, source_target_pairs={{0,24},{8,16},{16,8},{24,0},{1,25},{9,17},{17,9},{25,1},{2,26},{10... | collective-permute-start | bytes 1572872 | tf_op jit(solution)/shard_map/ppermute | solution.py:510
  (8 other events, 15.2 us)

commit v3 on v2

--- a/solution.py
+++ b/solution.py
@@ -22,10 +22,10 @@
     )
 
 
-def grad_kernel(G, F, NC, LAG, LEAD, owners, gain, x_hbm, cot_hbm, og, xbuf, gcol, scol, cotv, ga, ssall, res, *rest):
+def grad_kernel(G, F, NC, LAG, LEAD, owners, gain, x_hbm, cot_hbm, out, og, xbuf, gcol, scol, cotv, ga, ssall, res, *rest):
     nb = G.bit_length() - 1
     sends, recvs, curs = rest[:nb], rest[nb:2 * nb], rest[2 * nb:3 * nb - 1]
-    lsem, ss_send, ss_recv, go, gf, gr, rs_send, rs_recv = rest[3 * nb - 1:]
+    lsem, out_sem, ss_send, ss_recv, go, gf, gr, rs_send, rs_recv = rest[3 * nb - 1:]
     T, S = xbuf.shape
     N = cotv.shape[1]
     D = S * F
@@ -53,7 +53,7 @@
     for b in range(nb):
         pl.semaphore_signal(barrier, inc=1, device_id=(partner(b), f), device_id_type=MESH)
 
-    gcol[...] = jnp.broadcast_to(gain[...].astype(jnp.float32), (128, S)).T
+    gcol[...] = jnp.broadcast_to(gain[...].astype(jnp.float32)[None, :], (128, S)).T
     x_copy.wait()
     TT = 256
     for i in range(T // TT):
@@ -177,6 +177,10 @@
             for c, col, at in segments(h):
                 sends[0][k % 2, h, j, :, at:at + W] = res[k % (LAG + 1), slab_at(c, place), :, col:col + W]
         exchange(k, h, 0).start()
+
+    def emit(k, m):
+        rows = pl.ds(pl.multiple_of(m * S + k * rk, rk), rk)
+        return pltpu.make_async_copy(og.at[rows], out.at[rows], out_sem.at[k % 2, m])
 
     def receive(k, i):
         for h in range(2):
@@ -190,6 +194,13 @@
                     v = (v + recvs[i][k, h, 0, :, at:at + W].astype(jnp.float32)).astype(jnp.bfloat16)
                     for m in range(q):
                         og[pl.ds(pl.multiple_of(m * S + k * rk, rk), rk), col:col + W] = v[m * rk:(m + 1) * rk]
+                if h == 1:
+                    for m in range(q):
+                        @pl.when(k >= 2)
+                        def _():
+                            emit(k - 2, m).wait()
+
+                        emit(k, m).start()
                 continue
             reuse(k, h, i + 1)
             count = 1 << (nb - i - 2)
@@ -264,13 +275,15 @@
         ss_copy(f, (f + d) % F, d).wait_send()
     for k in range(NC - 2, NC):
         drain_gather(k)
+        for m in range(q):
+            emit(k, m).wait()
     for i in range(nb):
         for h in range(2):
             for k in (NC - 2, NC - 1):
                 exchange(k, h, i).wait_send()
 
 
-def gradient(G, F, owners, gain, x, cot, NC=16, LAG=1, LEAD=3):
+def gradient(G, F, owners, gain, x, cot, NC=32, LAG=3, LEAD=4):
     NC = min(NC, x.shape[1] // 16)
     T, S = x.shape
     N = cot.shape[1]
@@ -290,8 +303,9 @@
             pl.BlockSpec(memory_space=pl.ANY),
             pl.BlockSpec(memory_space=pl.ANY),
         ],
-        out_specs=pl.BlockSpec(memory_space=pltpu.VMEM),
+        out_specs=ANY,
         scratch_shapes=[
+            pltpu.VMEM((slab, N), bf),
             pltpu.VMEM((T, S), bf),
             pltpu.VMEM((S, 128), f32),
             pltpu.VMEM((T, 128), f32),
@@ -305,6 +319,7 @@
         + [pltpu.VMEM((LAG, 2, n, R, Nh), f32) for n in counts[1:]]
         + [
             dma((2,)),
+            dma((2, q)),
             dma((F - 1,)),
             dma((F,)),
             dma((RING, 5)),
@@ -318,7 +333,7 @@
         ),
         cost_estimate=pl.CostEstimate(flops=2 * T * S * F * N, bytes_accessed=2 * (T * S + T * N + slab * N), transcendentals=0),
         name="gradient_step",
-    )(owners, gain.reshape(1, S), x, cot)
+    )(owners, gain, x, cot)
 
 
 SCALE_EPSILON = 1e-06
@@ -335,11 +350,6 @@
 
 def dot(a, b, dims=(((1,), (0,)), ((), ()))):
     return lax.dot_general(a, b, dims, preferred_element_type=jnp.float32)
-
-
-def split(value):
-    high = value.astype(jnp.bfloat16)
-    return high, (value - high.astype(jnp.float32)).astype(jnp.bfloat16)
 
 
 def inverse_fourth_root(statistic):
@@ -363,11 +373,8 @@
     outs, held = rest[-G - 1:-1], rest[-1]
     me = lax.axis_index("group")
     grad = g_ref[...]
-    left_high, left_low = split(li_ref[...])
-    half = dot(left_high, grad) + dot(left_low, grad)
-    half_high, half_low = split(half)
-    right_high, right_low = split(ri_ref[...])
-    conditioned = dot(half_high, right_high) + dot(half_low, right_high) + dot(half_high, right_low)
+    half = dot(li_ref[...].astype(jnp.bfloat16), grad)
+    conditioned = dot(half.astype(jnp.bfloat16), ri_ref[...].astype(jnp.bfloat16))
     mean = jnp.sum(conditioned * conditioned, keepdims=True) * (1.0 / conditioned.size)
     held[...] = (conditioned * lax.rsqrt(mean + SCALE_EPSILON)).astype(jnp.bfloat16)
     rows = BLK // G
@@ -391,13 +398,13 @@
             dimension_semantics=("arbitrary",), vmem_limit_bytes=VMEM_LIMIT
         ),
         cost_estimate=pl.CostEstimate(
-            flops=(N // BLK) * 5 * 2 * BLK**3, bytes_accessed=(N // BLK) * 12 * BLK * BLK, transcendentals=0
+            flops=(N // BLK) * 2 * 2 * BLK**3, bytes_accessed=(N // BLK) * 12 * BLK * BLK, transcendentals=0
         ),
         name="condition_step",
     )(grad, left, right, *after)
 
 
-def stats_kernel(r, col_blocks, refresh, g_ref, ls_ref, rs_ref, li_ref, ri_ref, *rest):
+def stats_kernel(r, refresh, g_ref, ls_ref, rs_ref, li_ref, ri_ref, *rest):
     la_ref, ra_ref, ln_ref, rn_ref, token = rest[-5:]
     token[...] = jnp.zeros_like(token)
     grad = g_ref[...]
@@ -407,7 +414,7 @@
     ra_ref[...] = DECAY_RATE * rs_ref[...] + (1.0 - DECAY_RATE) * dot(
         grad, grad, (((0,), (0,)), ((), ()))
     )
-    flag = refresh[r * col_blocks + pl.program_id(0)]
+    flag = refresh[r, pl.program_id(0)]
 
     @pl.when(flag > 0)
     def _():
@@ -427,7 +434,7 @@
     held = [ANY] * (len(previous) + len(after))
     whole = jax.ShapeDtypeStruct((slab_rows, N), jnp.float32)
     return pl.pallas_call(
-        functools.partial(stats_kernel, r, col_blocks),
+        functools.partial(stats_kernel, r),
         grid_spec=pltpu.PrefetchScalarGridSpec(
             num_scalar_prefetch=1,
             grid=(col_blocks,),
@@ -453,7 +460,7 @@
     me = lax.axis_index("group")
     c = first + pl.program_id(0)
     for m in range(G):
-        wanted = owners[c * G + (me ^ m)] ^ me
+        wanted = owners[c, me ^ m] ^ me
         for k in range(G):
             @pl.when(wanted == k)
             def _():
@@ -514,7 +521,9 @@
 def cut(count, blocks):
     units = []
     for r in range(count):
-        cuts = [0, 1, blocks] if r == 0 and blocks > 1 else [0, blocks]
+        cuts = [0, blocks]
+        if blocks > 1 and r == 0:
+            cuts = [0, blocks // 2, blocks]
         units += [(r, lo, hi - lo) for lo, hi in zip(cuts, cuts[1:])]
     return units
 
@@ -522,7 +531,6 @@
 def body(G, F, inputs, norm_gain, cotangent, owners, refresh, *states):
     slab_rows, N = states[0].shape
     own = gradient(G, F, owners, norm_gain, inputs, cotangent)
-    flat_owners = owners.reshape(-1)
     count, blocks = slab_rows // BLK, N // BLK
     units = cut(count, blocks)
     sent, back, after = [], [], ()
@@ -532,11 +540,11 @@
         sent.append(swap(G, parts))
     previous = ()
     for r in range(count):
-        *previous, token = stats(r, own, refresh.reshape(-1), states, tuple(previous), after)
+        *previous, token = stats(r, own, refresh, states, tuple(previous), after)
         after = (token,)
         if r == 0:
             for unit, parts in zip(units, sent):
-                parts = relay(G, unit, flat_owners, parts, after)
+                parts = relay(G, unit, owners, parts, after)
                 after = (parts[0],)
                 back.append(swap(G, parts))
     update = ()

time: 305 us -> 291 us (0.954)
  Pallas kernels: 252 us -> 238 us
  local copies, waits for them, and re-layouts: 5.47 us -> 2.3 us
    pallas_call x1, Pallas kernels: 175 us -> 168 us  [gradient(): pl.pallas_call(functools.partial(grad_kernel, G, F, NC, LAG, LEAD), out_s...]
    pallas_call x3, Pallas kernels: 23.2 us -> 17.5 us  [condition(): pl.pallas_call(functools.partial(condition_kernel, G), grid=(N // BLK,),...]
  transfers between devices with their start and end apart: 18 -> 18, of which waited for: 4 -> 6; matrix products, arithmetic and copies ran while one was open for 0% -> 0% of each run, Pallas kernels for 20% -> 19%
where the time goes in v3:
time: 291 us; the launch traced here: 290 us
  Pallas kernels  238 us (82%)
  waiting for transfers between devices  26.7 us (9%)
  starting transfers between devices  22.7 us (8%)
    pallas_call x1, Pallas kernels, gradient(): pl.pallas_call(functools.partial(grad_kernel, G, F, NC, LAG, LEAD), out_s...  168 us
    pallas_call x2, Pallas kernels, stats(): pl.pallas_call(functools.partial(stats_kernel, r), grid_spec=pltpu.Prefet...  33 us
    ppermute x18, waiting for transfers between devices, swap(): out.append(lax.ppermute(parts[m], 'group', [(i, i ^ m) for i in range(G)]))  26.7 us
    ppermute x18, starting transfers between devices, swap(): out.append(lax.ppermute(parts[m], 'group', [(i, i ^ m) for i in range(G)]))  22.7 us
    pallas_call x3, Pallas kernels, condition(): pl.pallas_call(functools.partial(condition_kernel, G), grid=(N // BLK,),...  17.5 us
    pallas_call x3, Pallas kernels, relay(): pl.pallas_call(functools.partial(relay_kernel, G, unit[1]), grid_spec=plt...  10.6 us
    pallas_call x3, Pallas kernels, place(): pl.pallas_call(functools.partial(place_kernel, G), grid=(N // BLK,), in_s...  8.13 us
  transfers between devices with their start and end apart: 18, of which 6 were waited for; matrix products, arithmetic and copies ran while one was open for 0% of the time, Pallas kernels for 19%

profile of v3, /device:TPU:0, one launch (start us, length us, event | category | flops | bytes accessed | tf_op | source)
XLA Modules:
  0.0 290.1 jit_solution(5971283509334884919)
XLA Ops:
  0.6 168.4 %gradient_step.1.g_ref = bf16[1024,2048]{1,0:T(8,128)(2,1)} custom-call(s32[4,4]{1,0:T(4,128)} %owners.7, bf16[512]{0:T(512)(128)(2,1)} %gain.1, bf16[2048,512]{1,0:T(8,128)(2,1)} %x_hbm.1, bf16[2048,2048]{1,0:T(8,128)(2,1)} %cot_hbm.1), custom_call_target="tpu_custom_call" | custom-call | flops 34359738368 | bytes 14680064 | tf_op jit(solution)/shard_map/gradient_step/pallas_call | solution.py:297
  169.0 4.8 %condition_step.3 = (bf16[128,1024]{1,0:T(8,128)(2,1)}, bf16[128,1024]{1,0:T(8,128)(2,1)}, bf16[128,1024]{1,0:T(8,128)(2,1)}, bf16[128,1024]{1,0:T(8,128)(2,1)}) custom-call(bf16[1024,2048]{1,0:T(8,128)(2,1)} %gradient_step.1.g_ref, f32[1024,2048]{1,0:T(8,128)} %li_ref.9, f32[1024,2048]{1,0:T(8,128)} %ri_ref.9), custom_call_target="tpu_custom_call" | custom-call | flops 1073741824 | bytes 6291456 | tf_op jit(solution)/shard_map/condition_step/pallas_call | solution.py:390
  173.8 4.8 %condition_step.4 = (bf16[128,1024]{1,0:T(8,128)(2,1)}, bf16[128,1024]{1,0:T(8,128)(2,1)}, bf16[128,1024]{1,0:T(8,128)(2,1)}, bf16[128,1024]{1,0:T(8,128)(2,1)}) custom-call(bf16[1024,2048]{1,0:T(8,128)(2,1)} %gradient_step.1.g_ref, f32[1024,2048]{1,0:T(8,128)} %li_ref.9, f32[1024,2048]{1,0:T(8,128)} %ri_ref.9, ...), custom_call_target="tpu_custom_call" | custom-call | flops 1073741824 | bytes 6291456 | tf_op jit(solution)/shard_map/condition_step/pallas_call | solution.py:390
  178.6 1.5 collective-permute-start.3
  181.5 2.1 collective-permute-start.8
  183.6 7.9 %condition_step.5 = (bf16[128,2048]{1,0:T(8,128)(2,1)}, bf16[128,2048]{1,0:T(8,128)(2,1)}, bf16[128,2048]{1,0:T(8,128)(2,1)}, bf16[128,2048]{1,0:T(8,128)(2,1)}) custom-call(bf16[1024,2048]{1,0:T(8,128)(2,1)} %gradient_step.1.g_ref, f32[1024,2048]{1,0:T(8,128)} %li_ref.9, f32[1024,2048]{1,0:T(8,128)} %ri_ref.9, ...), custom_call_target="tpu_custom_call" | custom-call | flops 2147483648 | bytes 12582912 | tf_op jit(solution)/shard_map/condition_step/pallas_call | solution.py:390
  194.3 1.7 collective-permute-start.2
  197.3 2.4 collective-permute-done.8.refs_3_
  199.7 2.1 collective-permute-start.5
  201.8 16.4 %stats_step.2 = (f32[1024,2048]{1,0:T(8,128)}, f32[1024,2048]{1,0:T(8,128)}, f32[1024,2048]{1,0:T(8,128)}, f32[1024,2048]{1,0:T(8,128)}, f32[8,128]{1,0:T(8,128)}) custom-call(s32[2,4]{1,0:T(2,128)} %refresh.3, bf16[1024,2048]{1,0:T(8,128)(2,1)} %gradient_step.1.g_ref, f32[1024,2048]{1,0:T(8,128)} %ls_ref.3, f32[1024,2048]{1,0:T(8,128)} %rs_ref.3, ...), custom_call_target="tpu_custom_call" | custom-call | flops 8589934592 | bytes 37748736 | tf_op jit(solution)/shard_map/stats_step/pallas_call | solution.py:436
  218.2 3.0 %relay_step.3 = (bf16[128,1024]{1,0:T(8,128)(2,1)}, bf16[128,1024]{1,0:T(8,128)(2,1)}, bf16[128,1024]{1,0:T(8,128)(2,1)}, bf16[128,1024]{1,0:T(8,128)(2,1)}) custom-call(s32[4,4]{1,0:T(4,128)} %owners.7, bf16[128,1024]{1,0:T(8,128)(2,1)} %get-tuple-element.39.rest_0_.refs_0_, bf16[128,1024]{1,0:T(8,128)(2,1)} %copy-done.8, ...), custom_call_target="tpu_custom_call" | custom-call | bytes 2097152 | tf_op jit(solution)/shard_map/relay_step/pallas_call | solution.py:473
  221.2 11.3 %collective-permute-done.4.refs_2_ = bf16[128,1024]{1,0:T(8,128)(2,1)} collective-permute-done((bf16[128,1024]{1,0:T(8,128)(2,1)}, bf16[128,1024]{1,0:T(8,128)(2,1)}, u32[]{:S(2)}, u32[]{:S(2)}) %collective-permute-start.4) | collective-permute-done | bytes 262176 | tf_op jit(solution)/shard_map/ppermute | solution.py:517
  232.5 2.9 %relay_step.4 = (bf16[128,1024]{1,0:T(8,128)(2,1)}, bf16[128,1024]{1,0:T(8,128)(2,1)}, bf16[128,1024]{1,0:T(8,128)(2,1)}, bf16[128,1024]{1,0:T(8,128)(2,1)}) custom-call(s32[4,4]{1,0:T(4,128)} %owners.7, bf16[128,1024]{1,0:T(8,128)(2,1)} %get-tuple-element.40.rest_0_.refs_0_, bf16[128,1024]{1,0:T(8,128)(2,1)} %copy-done.7, ...), custom_call_target="tpu_custom_call" | custom-call | bytes 2097152 | tf_op jit(solution)/shard_map/relay_step/pallas_call | solution.py:473
  235.5 1.3 collective-permute-start.12
  238.6 1.7 collective-permute-start.17
  241.4 4.7 %relay_step.5 = (bf16[128,2048]{1,0:T(8,128)(2,1)}, bf16[128,2048]{1,0:T(8,128)(2,1)}, bf16[128,2048]{1,0:T(8,128)(2,1)}, bf16[128,2048]{1,0:T(8,128)(2,1)}) custom-call(s32[4,4]{1,0:T(4,128)} %owners.7, bf16[128,2048]{1,0:T(8,128)(2,1)} %get-tuple-element.41.rest_0_.refs_0_, bf16[128,2048]{1,0:T(8,128)(2,1)} %copy-done.3, bf16[128,2048]{1,0:T(8,128)(2,1)} %copy-done.4, ...), custom_call_target="tpu_custom_call" | custom-call | bytes 4194304 | tf_op jit(solution)/shard_map/relay_step/pallas_call | solution.py:473
  247.3 3.3 %collective-permute-done.15.refs_1_ = bf16[128,1024]{1,0:T(8,128)(2,1)} collective-permute-done((bf16[128,1024]{1,0:T(8,128)(2,1)}, bf16[128,1024]{1,0:T(8,128)(2,1)}, u32[]{:S(2)}, u32[]{:S(2)}) %collective-permute-start.15) | collective-permute-done | bytes 262176 | tf_op jit(solution)/shard_map/ppermute | solution.py:517
  253.1 3.8 %collective-permute-done.17.refs_3_ = bf16[128,1024]{1,0:T(8,128)(2,1)} collective-permute-done((bf16[128,1024]{1,0:T(8,128)(2,1)}, bf16[128,1024]{1,0:T(8,128)(2,1)}, u32[]{:S(2)}, u32[]{:S(2)}) %collective-permute-start.17) | collective-permute-done | bytes 262176 | tf_op jit(solution)/shard_map/ppermute | solution.py:517
  256.8 1.7 collective-permute-start.11
  258.6 16.6 %stats_step.3 = (f32[1024,2048]{1,0:T(8,128)}, f32[1024,2048]{1,0:T(8,128)}, f32[1024,2048]{1,0:T(8,128)}, f32[1024,2048]{1,0:T(8,128)}, f32[8,128]{1,0:T(8,128)}) custom-call(s32[2,4]{1,0:T(2,128)} %refresh.3, bf16[1024,2048]{1,0:T(8,128)(2,1)} %gradient_step.1.g_ref, ...), custom_call_target="tpu_custom_call", output_to_operand_aliasing={{0}: (6, {}), {1}: (7, {}), {2}: (8, {}), {3}: (9, {})} | custom-call | flops 8589934592 | bytes 37748736 | tf_op jit(solution)/shard_map/stats_step/pallas_call | solution.py:436
  275.2 2.1 place_step.3.refs_4_
  277.3 2.2 place_step.4.refs_4_
  279.5 5.2 %collective-permute-done.10.refs_2_ = bf16[128,2048]{1,0:T(8,128)(2,1)S(1)} collective-permute-done((bf16[128,2048]{1,0:T(8,128)(2,1)}, bf16[128,2048]{1,0:T(8,128)(2,1)S(1)}, u32[]{:S(2)}, u32[]{:S(2)}) %collective-permute-start.10) | collective-permute-done | bytes 524320 | tf_op jit(solution)/shard_map/ppermute | solution.py:517
  286.3 3.8 %place_step.5 = bf16[1024,2048]{1,0:T(8,128)(2,1)} custom-call(bf16[128,2048]{1,0:T(8,128)(2,1)} %get-tuple-element.54.rest_4_.refs_0_, bf16[128,2048]{1,0:T(8,128)(2,1)} %copy-done, bf16[128,2048]{1,0:T(8,128)(2,1)} %copy-done.1, bf16[128,2048]{1,0:T(8,128)(2,1)} %copy-done.2, ...), custom_call_target="tpu_custom_call", output_to_operand_aliasing={{}: (4, {})} | custom-call | bytes 4194304 | tf_op jit(solution)/shard_map/place_step/pallas_call | solution.py:499
  (44 shorter events, 13.4 us)
Async XLA Ops:
  173.8 6.3 %copy-start.9 = (bf16[128,1024]{1,0:T(8,128)(2,1)S(1)}, bf16[128,1024]{1,0:T(8,128)(2,1)}, u32[]{:S(2)}) copy-start(bf16[128,1024]{1,0:T(8,128)(2,1)} %get-tuple-element.48) | copy-start | bytes 786436
  178.6 13.5 %collective-permute-start.3 = (bf16[128,1024]{1,0:T(8,128)(2,1)}, bf16[128,1024]{1,0:T(8,128)(2,1)S(1)}, u32[]{:S(2)}, u32[]{:S(2)}) collective-permute-start(bf16[128,1024]{1,0:T(8,128)(2,1)} %get-tuple-element.45), channel_id=1, source_target_pairs={{0,8},{8,0},{16,24},{24,16},{1,9},{9,1},{17,25},{25,17},{2,10},{10... | collective-permute-start | bytes 786440 | tf_op jit(solution)/shard_map/ppermute | solution.py:517
  180.1 13.5 %collective-permute-start.6 = (bf16[128,1024]{1,0:T(8,128)(2,1)S(1)}, bf16[128,1024]{1,0:T(8,128)(2,1)S(1)}, u32[]{:S(2)}, u32[]{:S(2)}) collective-permute-start(bf16[128,1024]{1,0:T(8,128)(2,1)S(1)} %copy-done.9), channel_id=1, source_target_pairs={{0,8},{8,0},{16,24},{24,16},{1,9},{9,1},{17,25},{25,17},{2,10},{10... | collective-permute-start | bytes 786440 | tf_op jit(solution)/shard_map/ppermute | solution.py:517
  180.7 15.3 %collective-permute-start.7 = (bf16[128,1024]{1,0:T(8,128)(2,1)}, bf16[128,1024]{1,0:T(8,128)(2,1)}, u32[]{:S(2)}, u32[]{:S(2)}) collective-permute-start(bf16[128,1024]{1,0:T(8,128)(2,1)} %get-tuple-element.49), channel_id=1, source_target_pairs={{0,16},{8,24},{16,0},{24,8},{1,17},{9,25},{17,1},{25,9},{2,18},{10... | collective-permute-start | bytes 786440 | tf_op jit(solution)/shard_map/ppermute | solution.py:517
  181.5 18.2 %collective-permute-start.8 = (bf16[128,1024]{1,0:T(8,128)(2,1)}, bf16[128,1024]{1,0:T(8,128)(2,1)}, u32[]{:S(2)}, u32[]{:S(2)}) collective-permute-start(bf16[128,1024]{1,0:T(8,128)(2,1)} %get-tuple-element.50), channel_id=1, source_target_pairs={{0,24},{8,16},{16,8},{24,0},{1,25},{9,17},{17,9},{25,1},{2,26},{10... | collective-permute-start | bytes 786440 | tf_op jit(solution)/shard_map/ppermute | solution.py:517
  191.6 45.9 %collective-permute-start = (bf16[128,2048]{1,0:T(8,128)(2,1)}, bf16[128,2048]{1,0:T(8,128)(2,1)S(1)}, u32[]{:S(2)}, u32[]{:S(2)}) collective-permute-start(bf16[128,2048]{1,0:T(8,128)(2,1)} %get-tuple-element.42), channel_id=1, source_target_pairs={{0,8},{8,0},{16,24},{24,16},{1,9},{9,1},{17,25},{25,17},{2,10},{10... | collective-permute-start | bytes 1572872 | tf_op jit(solution)/shard_map/ppermute | solution.py:517
  192.1 26.1 %copy-start.7 = (bf16[128,1024]{1,0:T(8,128)(2,1)}, bf16[128,1024]{1,0:T(8,128)(2,1)S(1)}, u32[]{:S(2)}) copy-start(bf16[128,1024]{1,0:T(8,128)(2,1)S(1)} %collective-permute-done.3.refs_1_) | copy-start | bytes 786436
  192.1 46.5 %collective-permute-start.1 = (bf16[128,2048]{1,0:T(8,128)(2,1)}, bf16[128,2048]{1,0:T(8,128)(2,1)S(1)}, u32[]{:S(2)}, u32[]{:S(2)}) collective-permute-start(bf16[128,2048]{1,0:T(8,128)(2,1)} %get-tuple-element.43), channel_id=1, source_target_pairs={{0,16},{8,24},{16,0},{24,8},{1,17},{9,25},{17,1},{25,9},{2,18},{10... | collective-permute-start | bytes 1572872 | tf_op jit(solution)/shard_map/ppermute | solution.py:517
  194.3 46.0 %collective-permute-start.2 = (bf16[128,2048]{1,0:T(8,128)(2,1)}, bf16[128,2048]{1,0:T(8,128)(2,1)S(1)}, u32[]{:S(2)}, u32[]{:S(2)}) collective-permute-start(bf16[128,2048]{1,0:T(8,128)(2,1)} %get-tuple-element.44), channel_id=1, source_target_pairs={{0,24},{8,16},{16,8},{24,0},{1,25},{9,17},{17,9},{25,1},{2,26},{10... | collective-permute-start | bytes 1572872 | tf_op jit(solution)/shard_map/ppermute | solution.py:517
  196.0 36.5 %collective-permute-start.4 = (bf16[128,1024]{1,0:T(8,128)(2,1)}, bf16[128,1024]{1,0:T(8,128)(2,1)}, u32[]{:S(2)}, u32[]{:S(2)}) collective-permute-start(bf16[128,1024]{1,0:T(8,128)(2,1)} %get-tuple-element.46), channel_id=1, source_target_pairs={{0,16},{8,24},{16,0},{24,8},{1,17},{9,25},{17,1},{25,9},{2,18},{10... | collective-permute-start | bytes 786440 | tf_op jit(solution)/shard_map/ppermute | solution.py:517
  199.7 32.9 %collective-permute-start.5 = (bf16[128,1024]{1,0:T(8,128)(2,1)}, bf16[128,1024]{1,0:T(8,128)(2,1)}, u32[]{:S(2)}, u32[]{:S(2)}) collective-permute-start(bf16[128,1024]{1,0:T(8,128)(2,1)} %get-tuple-element.47), channel_id=1, source_target_pairs={{0,24},{8,16},{16,8},{24,0},{1,25},{9,17},{17,9},{25,1},{2,26},{10... | collective-permute-start | bytes 786440 | tf_op jit(solution)/shard_map/ppermute | solution.py:517
  235.5 10.7 %collective-permute-start.12 = (bf16[128,1024]{1,0:T(8,128)(2,1)}, bf16[128,1024]{1,0:T(8,128)(2,1)S(1)}, u32[]{:S(2)}, u32[]{:S(2)}) collective-permute-start(bf16[128,1024]{1,0:T(8,128)(2,1)} %get-tuple-element.58), channel_id=1, source_target_pairs={{0,8},{8,0},{16,24},{24,16},{1,9},{9,1},{17,25},{25,17},{2,10},{10... | collective-permute-start | bytes 786440 | tf_op jit(solution)/shard_map/ppermute | solution.py:517
  236.8 13.8 %collective-permute-start.15 = (bf16[128,1024]{1,0:T(8,128)(2,1)}, bf16[128,1024]{1,0:T(8,128)(2,1)}, u32[]{:S(2)}, u32[]{:S(2)}) collective-permute-start(bf16[128,1024]{1,0:T(8,128)(2,1)} %get-tuple-element.61), channel_id=1, source_target_pairs={{0,8},{8,0},{16,24},{24,16},{1,9},{9,1},{17,25},{25,17},{2,10},{10... | collective-permute-start | bytes 786440 | tf_op jit(solution)/shard_map/ppermute | solution.py:517
  237.5 3.9 %copy-start.3 = (bf16[128,2048]{1,0:T(8,128)(2,1)}, bf16[128,2048]{1,0:T(8,128)(2,1)S(1)}, u32[]{:S(2)}) copy-start(bf16[128,2048]{1,0:T(8,128)(2,1)S(1)} %collective-permute-done.refs_1_) | copy-start | bytes 1572868
  237.5 14.4 %collective-permute-start.16 = (bf16[128,1024]{1,0:T(8,128)(2,1)}, bf16[128,1024]{1,0:T(8,128)(2,1)}, u32[]{:S(2)}, u32[]{:S(2)}) collective-permute-start(bf16[128,1024]{1,0:T(8,128)(2,1)} %get-tuple-element.62), channel_id=1, source_target_pairs={{0,16},{8,24},{16,0},{24,8},{1,17},{9,25},{17,1},{25,9},{2,18},{10... | collective-permute-start | bytes 786440 | tf_op jit(solution)/shard_map/ppermute | solution.py:517
  238.6 2.9 copy-start.4
  238.6 18.2 %collective-permute-start.17 = (bf16[128,1024]{1,0:T(8,128)(2,1)}, bf16[128,1024]{1,0:T(8,128)(2,1)}, u32[]{:S(2)}, u32[]{:S(2)}) collective-permute-start(bf16[128,1024]{1,0:T(8,128)(2,1)} %get-tuple-element.63), channel_id=1, source_target_pairs={{0,24},{8,16},{16,8},{24,0},{1,25},{9,17},{17,9},{25,1},{2,26},{10... | collective-permute-start | bytes 786440 | tf_op jit(solution)/shard_map/ppermute | solution.py:517
  240.3 37.0 %collective-permute-start.13 = (bf16[128,1024]{1,0:T(8,128)(2,1)}, bf16[128,1024]{1,0:T(8,128)(2,1)}, u32[]{:S(2)}, u32[]{:S(2)}) collective-permute-start(bf16[128,1024]{1,0:T(8,128)(2,1)} %get-tuple-element.59), channel_id=1, source_target_pairs={{0,16},{8,24},{16,0},{24,8},{1,17},{9,25},{17,1},{25,9},{2,18},{10... | collective-permute-start | bytes 786440 | tf_op jit(solution)/shard_map/ppermute | solution.py:517
  246.2 29.0 %copy-start.6 = (bf16[128,1024]{1,0:T(8,128)(2,1)}, bf16[128,1024]{1,0:T(8,128)(2,1)S(1)}, u32[]{:S(2)}) copy-start(bf16[128,1024]{1,0:T(8,128)(2,1)S(1)} %collective-permute-done.12.refs_1_) | copy-start | bytes 786436
  246.2 31.1 %collective-permute-start.14 = (bf16[128,1024]{1,0:T(8,128)(2,1)}, bf16[128,1024]{1,0:T(8,128)(2,1)}, u32[]{:S(2)}, u32[]{:S(2)}) collective-permute-start(bf16[128,1024]{1,0:T(8,128)(2,1)} %get-tuple-element.60), channel_id=1, source_target_pairs={{0,24},{8,16},{16,8},{24,0},{1,25},{9,17},{17,9},{25,1},{2,26},{10... | collective-permute-start | bytes 786440 | tf_op jit(solution)/shard_map/ppermute | solution.py:517
  250.6 28.9 %collective-permute-start.9 = (bf16[128,2048]{1,0:T(8,128)(2,1)}, bf16[128,2048]{1,0:T(8,128)(2,1)S(1)}, u32[]{:S(2)}, u32[]{:S(2)}) collective-permute-start(bf16[128,2048]{1,0:T(8,128)(2,1)} %get-tuple-element.55), channel_id=1, source_target_pairs={{0,8},{8,0},{16,24},{24,16},{1,9},{9,1},{17,25},{25,17},{2,10},{10... | collective-permute-start | bytes 1572872 | tf_op jit(solution)/shard_map/ppermute | solution.py:517
  251.9 32.7 %collective-permute-start.10 = (bf16[128,2048]{1,0:T(8,128)(2,1)}, bf16[128,2048]{1,0:T(8,128)(2,1)S(1)}, u32[]{:S(2)}, u32[]{:S(2)}) collective-permute-start(bf16[128,2048]{1,0:T(8,128)(2,1)} %get-tuple-element.56), channel_id=1, source_target_pairs={{0,16},{8,24},{16,0},{24,8},{1,17},{9,25},{17,1},{25,9},{2,18},{10... | collective-permute-start | bytes 1572872 | tf_op jit(solution)/shard_map/ppermute | solution.py:517
  256.8 27.9 %collective-permute-start.11 = (bf16[128,2048]{1,0:T(8,128)(2,1)}, bf16[128,2048]{1,0:T(8,128)(2,1)S(1)}, u32[]{:S(2)}, u32[]{:S(2)}) collective-permute-start(bf16[128,2048]{1,0:T(8,128)(2,1)} %get-tuple-element.57), channel_id=1, source_target_pairs={{0,24},{8,16},{16,8},{24,0},{1,25},{9,17},{17,9},{25,1},{2,26},{10... | collective-permute-start | bytes 1572872 | tf_op jit(solution)/shard_map/ppermute | solution.py:517
  279.5 5.2 %copy-start = (bf16[128,2048]{1,0:T(8,128)(2,1)}, bf16[128,2048]{1,0:T(8,128)(2,1)S(1)}, u32[]{:S(2)}) copy-start(bf16[128,2048]{1,0:T(8,128)(2,1)S(1)} %collective-permute-done.9.refs_1_) | copy-start | bytes 1572868
  (4 other events, 3.4 us)

commit v4 on v3

--- a/solution.py
+++ b/solution.py
@@ -10,6 +10,7 @@
 BLK = 512
 ANY = pl.BlockSpec(memory_space=pl.ANY)
 VMEM_LIMIT = 62 * 1024 * 1024
+VMEM_ALL = 67043328
 NORM_EPSILON = 1e-05
 MESH = pl.DeviceIdType.MESH
 RING = 8
@@ -395,7 +396,7 @@
         out_shape=[jax.ShapeDtypeStruct((BLK // G, N), jnp.bfloat16)] * G,
         scratch_shapes=[pltpu.VMEM((BLK, BLK), jnp.bfloat16)],
         compiler_params=pltpu.CompilerParams(
-            dimension_semantics=("arbitrary",), vmem_limit_bytes=VMEM_LIMIT
+            dimension_semantics=("arbitrary",), vmem_limit_bytes=VMEM_ALL
         ),
         cost_estimate=pl.CostEstimate(
             flops=(N // BLK) * 2 * 2 * BLK**3, bytes_accessed=(N // BLK) * 12 * BLK * BLK, transcendentals=0
@@ -444,7 +445,7 @@
         out_shape=[whole] * 4 + [jax.ShapeDtypeStruct((8, 128), jnp.float32)],
         input_output_aliases={6 + i: i for i in range(len(previous))},
         compiler_params=pltpu.CompilerParams(
-            dimension_semantics=("arbitrary",), vmem_limit_bytes=VMEM_LIMIT
+            dimension_semantics=("arbitrary",), vmem_limit_bytes=VMEM_ALL
         ),
         cost_estimate=pl.CostEstimate(
             flops=col_blocks * 8 * 2 * BLK**3,
@@ -477,7 +478,7 @@
         ),
         out_shape=[jax.ShapeDtypeStruct((rows, N), jnp.bfloat16)] * G,
         compiler_params=pltpu.CompilerParams(
-            dimension_semantics=("arbitrary",), vmem_limit_bytes=VMEM_LIMIT
+            dimension_semantics=("arbitrary",), vmem_limit_bytes=VMEM_ALL
         ),
         cost_estimate=pl.CostEstimate(flops=0, bytes_accessed=4 * G * rows * N, transcendentals=0),
         name="relay_step",
@@ -495,16 +496,18 @@
 def place(G, unit, shape, parts, previous, after):
     rows, N = parts[0].shape
     r, first = unit[:2]
-    part = pl.BlockSpec((rows, BLK), lambda c: (0, c))
+    wide = BLK * (2 if N % (2 * BLK) == 0 and first % 2 == 0 else 1)
+    start = first * BLK // wide
+    part = pl.BlockSpec((rows, wide), lambda c: (0, c))
     return pl.pallas_call(
         functools.partial(place_kernel, G),
-        grid=(N // BLK,),
+        grid=(N // wide,),
         in_specs=[part] * G + [ANY] * (len(previous) + len(after)),
-        out_specs=pl.BlockSpec((BLK, BLK), lambda c: (r, first + c)),
+        out_specs=pl.BlockSpec((BLK, wide), lambda c: (r, start + c)),
         out_shape=jax.ShapeDtypeStruct(shape, jnp.bfloat16),
         input_output_aliases={G: 0} if previous else {},
         compiler_params=pltpu.CompilerParams(
-            dimension_semantics=("arbitrary",), vmem_limit_bytes=VMEM_LIMIT
+            dimension_semantics=("arbitrary",), vmem_limit_bytes=VMEM_ALL
         ),
         cost_estimate=pl.CostEstimate(flops=0, bytes_accessed=4 * BLK * N, transcendentals=0),
         name="place_step",

time: 291 us -> 288 us (0.990)
  transfers between devices with their start and end apart: 18 -> 18, of which waited for: 6 -> 6; matrix products, arithmetic and copies ran while one was open for 0% -> 0% of each run, Pallas kernels for 19% -> 20%
where the time goes in v4:
time: 288 us; the launch traced here: 287 us
  Pallas kernels  237 us (82%)
  waiting for transfers between devices  27.2 us (9%)
  starting transfers between devices  22.7 us (8%)
    pallas_call x1, Pallas kernels, gradient(): pl.pallas_call(functools.partial(grad_kernel, G, F, NC, LAG, LEAD), out_s...  168 us
    pallas_call x2, Pallas kernels, stats(): pl.pallas_call(functools.partial(stats_kernel, r), grid_spec=pltpu.Prefet...  33.1 us
    ppermute x18, waiting for transfers between devices, swap(): out.append(lax.ppermute(parts[m], 'group', [(i, i ^ m) for i in range(G)]))  27.2 us
    ppermute x18, starting transfers between devices, swap(): out.append(lax.ppermute(parts[m], 'group', [(i, i ^ m) for i in range(G)]))  22.7 us
    pallas_call x3, Pallas kernels, condition(): pl.pallas_call(functools.partial(condition_kernel, G), grid=(N // BLK,),...  17.4 us
    pallas_call x3, Pallas kernels, relay(): pl.pallas_call(functools.partial(relay_kernel, G, unit[1]), grid_spec=plt...  10.6 us
    pallas_call x3, Pallas kernels, place(): pl.pallas_call(functools.partial(place_kernel, G), grid=(N // wide,), in_...  7.06 us
  transfers between devices with their start and end apart: 18, of which 6 were waited for; matrix products, arithmetic and copies ran while one was open for 0% of the time, Pallas kernels for 20%

profile of v4, /device:TPU:0, one launch (start us, length us, event | category | flops | bytes accessed | tf_op | source)
XLA Modules:
  0.0 287.2 jit_solution(13581573365137234899)
XLA Ops:
  0.6 168.4 %gradient_step.1.g_ref = bf16[1024,2048]{1,0:T(8,128)(2,1)} custom-call(s32[4,4]{1,0:T(4,128)} %owners.7, bf16[512]{0:T(512)(128)(2,1)} %gain.1, bf16[2048,512]{1,0:T(8,128)(2,1)} %x_hbm.1, bf16[2048,2048]{1,0:T(8,128)(2,1)} %cot_hbm.1), custom_call_target="tpu_custom_call" | custom-call | flops 34359738368 | bytes 14680064 | tf_op jit(solution)/shard_map/gradient_step/pallas_call | solution.py:298
  169.0 4.8 %condition_step.3 = (bf16[128,1024]{1,0:T(8,128)(2,1)}, bf16[128,1024]{1,0:T(8,128)(2,1)}, bf16[128,1024]{1,0:T(8,128)(2,1)}, bf16[128,1024]{1,0:T(8,128)(2,1)}) custom-call(bf16[1024,2048]{1,0:T(8,128)(2,1)} %gradient_step.1.g_ref, f32[1024,2048]{1,0:T(8,128)} %li_ref.9, f32[1024,2048]{1,0:T(8,128)} %ri_ref.9), custom_call_target="tpu_custom_call" | custom-call | flops 1073741824 | bytes 6291456 | tf_op jit(solution)/shard_map/condition_step/pallas_call | solution.py:391
  173.8 4.8 %condition_step.4 = (bf16[128,1024]{1,0:T(8,128)(2,1)}, bf16[128,1024]{1,0:T(8,128)(2,1)}, bf16[128,1024]{1,0:T(8,128)(2,1)}, bf16[128,1024]{1,0:T(8,128)(2,1)}) custom-call(bf16[1024,2048]{1,0:T(8,128)(2,1)} %gradient_step.1.g_ref, f32[1024,2048]{1,0:T(8,128)} %li_ref.9, f32[1024,2048]{1,0:T(8,128)} %ri_ref.9, ...), custom_call_target="tpu_custom_call" | custom-call | flops 1073741824 | bytes 6291456 | tf_op jit(solution)/shard_map/condition_step/pallas_call | solution.py:391
  178.5 1.5 collective-permute-start.3
  181.4 2.1 collective-permute-start.8
  183.5 7.9 %condition_step.5 = (bf16[128,2048]{1,0:T(8,128)(2,1)}, bf16[128,2048]{1,0:T(8,128)(2,1)}, bf16[128,2048]{1,0:T(8,128)(2,1)}, bf16[128,2048]{1,0:T(8,128)(2,1)}) custom-call(bf16[1024,2048]{1,0:T(8,128)(2,1)} %gradient_step.1.g_ref, f32[1024,2048]{1,0:T(8,128)} %li_ref.9, f32[1024,2048]{1,0:T(8,128)} %ri_ref.9, ...), custom_call_target="tpu_custom_call" | custom-call | flops 2147483648 | bytes 12582912 | tf_op jit(solution)/shard_map/condition_step/pallas_call | solution.py:391
  193.7 1.7 collective-permute-start.2
  196.6 3.0 %collective-permute-done.8.refs_3_ = bf16[128,1024]{1,0:T(8,128)(2,1)} collective-permute-done((bf16[128,1024]{1,0:T(8,128)(2,1)}, bf16[128,1024]{1,0:T(8,128)(2,1)}, u32[]{:S(2)}, u32[]{:S(2)}) %collective-permute-start.8) | collective-permute-done | bytes 262176 | tf_op jit(solution)/shard_map/ppermute | solution.py:520
  199.6 2.1 collective-permute-start.5
  201.7 16.5 %stats_step.2 = (f32[1024,2048]{1,0:T(8,128)}, f32[1024,2048]{1,0:T(8,128)}, f32[1024,2048]{1,0:T(8,128)}, f32[1024,2048]{1,0:T(8,128)}, f32[8,128]{1,0:T(8,128)}) custom-call(s32[2,4]{1,0:T(2,128)} %refresh.3, bf16[1024,2048]{1,0:T(8,128)(2,1)} %gradient_step.1.g_ref, f32[1024,2048]{1,0:T(8,128)} %ls_ref.3, f32[1024,2048]{1,0:T(8,128)} %rs_ref.3, ...), custom_call_target="tpu_custom_call" | custom-call | flops 8589934592 | bytes 37748736 | tf_op jit(solution)/shard_map/stats_step/pallas_call | solution.py:437
  218.2 3.0 %relay_step.3 = (bf16[128,1024]{1,0:T(8,128)(2,1)}, bf16[128,1024]{1,0:T(8,128)(2,1)}, bf16[128,1024]{1,0:T(8,128)(2,1)}, bf16[128,1024]{1,0:T(8,128)(2,1)}) custom-call(s32[4,4]{1,0:T(4,128)} %owners.7, bf16[128,1024]{1,0:T(8,128)(2,1)} %get-tuple-element.39.rest_0_.refs_0_, bf16[128,1024]{1,0:T(8,128)(2,1)} %collective-permute-done.6.refs_1_, ...), custom_call_target="tpu_custom_call" | custom-call | bytes 2097152 | tf_op jit(solution)/shard_map/relay_step/pallas_call | solution.py:474
  221.1 11.3 %collective-permute-done.4.refs_2_ = bf16[128,1024]{1,0:T(8,128)(2,1)} collective-permute-done((bf16[128,1024]{1,0:T(8,128)(2,1)}, bf16[128,1024]{1,0:T(8,128)(2,1)}, u32[]{:S(2)}, u32[]{:S(2)}) %collective-permute-start.4) | collective-permute-done | bytes 262176 | tf_op jit(solution)/shard_map/ppermute | solution.py:520
  232.4 2.9 %relay_step.4 = (bf16[128,1024]{1,0:T(8,128)(2,1)}, bf16[128,1024]{1,0:T(8,128)(2,1)}, bf16[128,1024]{1,0:T(8,128)(2,1)}, bf16[128,1024]{1,0:T(8,128)(2,1)}) custom-call(s32[4,4]{1,0:T(4,128)} %owners.7, bf16[128,1024]{1,0:T(8,128)(2,1)} %get-tuple-element.40.rest_0_.refs_0_, bf16[128,1024]{1,0:T(8,128)(2,1)} %collective-permute-done.3.refs_1_, ...), custom_call_target="tpu_custom_call" | custom-call | bytes 2097152 | tf_op jit(solution)/shard_map/relay_step/pallas_call | solution.py:474
  235.4 1.4 collective-permute-start.12
  238.5 1.8 collective-permute-start.17
  241.3 4.8 %relay_step.5 = (bf16[128,2048]{1,0:T(8,128)(2,1)}, bf16[128,2048]{1,0:T(8,128)(2,1)}, bf16[128,2048]{1,0:T(8,128)(2,1)}, bf16[128,2048]{1,0:T(8,128)(2,1)}) custom-call(s32[4,4]{1,0:T(4,128)} %owners.7, bf16[128,2048]{1,0:T(8,128)(2,1)} %get-tuple-element.41.rest_0_.refs_0_, bf16[128,2048]{1,0:T(8,128)(2,1)} %collective-permute-done.refs_1_, ...), custom_call_target="tpu_custom_call" | custom-call | bytes 4194304 | tf_op jit(solution)/shard_map/relay_step/pallas_call | solution.py:474
  247.2 3.3 %collective-permute-done.15.refs_1_ = bf16[128,1024]{1,0:T(8,128)(2,1)} collective-permute-done((bf16[128,1024]{1,0:T(8,128)(2,1)}, bf16[128,1024]{1,0:T(8,128)(2,1)}, u32[]{:S(2)}, u32[]{:S(2)}) %collective-permute-start.15) | collective-permute-done | bytes 262176 | tf_op jit(solution)/shard_map/ppermute | solution.py:520
  252.9 3.8 %collective-permute-done.17.refs_3_ = bf16[128,1024]{1,0:T(8,128)(2,1)} collective-permute-done((bf16[128,1024]{1,0:T(8,128)(2,1)}, bf16[128,1024]{1,0:T(8,128)(2,1)}, u32[]{:S(2)}, u32[]{:S(2)}) %collective-permute-start.17) | collective-permute-done | bytes 262176 | tf_op jit(solution)/shard_map/ppermute | solution.py:520
  256.7 1.8 collective-permute-start.11
  258.4 16.6 %stats_step.3 = (f32[1024,2048]{1,0:T(8,128)}, f32[1024,2048]{1,0:T(8,128)}, f32[1024,2048]{1,0:T(8,128)}, f32[1024,2048]{1,0:T(8,128)}, f32[8,128]{1,0:T(8,128)}) custom-call(s32[2,4]{1,0:T(2,128)} %refresh.3, bf16[1024,2048]{1,0:T(8,128)(2,1)} %gradient_step.1.g_ref, ...), custom_call_target="tpu_custom_call", output_to_operand_aliasing={{0}: (6, {}), {1}: (7, {}), {2}: (8, {}), {3}: (9, {})} | custom-call | flops 8589934592 | bytes 37748736 | tf_op jit(solution)/shard_map/stats_step/pallas_call | solution.py:437
  275.0 2.2 place_step.3.refs_4_
  277.3 2.2 place_step.4.refs_4_
  279.5 5.1 %collective-permute-done.10.refs_2_ = bf16[128,2048]{1,0:T(8,128)(2,1)} collective-permute-done((bf16[128,2048]{1,0:T(8,128)(2,1)}, bf16[128,2048]{1,0:T(8,128)(2,1)}, u32[]{:S(2)}, u32[]{:S(2)}) %collective-permute-start.10) | collective-permute-done | bytes 524320 | tf_op jit(solution)/shard_map/ppermute | solution.py:520
  284.6 2.6 place_step.5
  (24 shorter events, 11.3 us)
Async XLA Ops:
  178.5 13.5 %collective-permute-start.3 = (bf16[128,1024]{1,0:T(8,128)(2,1)}, bf16[128,1024]{1,0:T(8,128)(2,1)}, u32[]{:S(2)}, u32[]{:S(2)}) collective-permute-start(bf16[128,1024]{1,0:T(8,128)(2,1)} %get-tuple-element.45), channel_id=1, source_target_pairs={{0,8},{8,0},{16,24},{24,16},{1,9},{9,1},{17,25},{25,17},{2,10},{10... | collective-permute-start | bytes 786440 | tf_op jit(solution)/shard_map/ppermute | solution.py:520
  180.0 13.6 %collective-permute-start.6 = (bf16[128,1024]{1,0:T(8,128)(2,1)}, bf16[128,1024]{1,0:T(8,128)(2,1)}, u32[]{:S(2)}, u32[]{:S(2)}) collective-permute-start(bf16[128,1024]{1,0:T(8,128)(2,1)} %get-tuple-element.48), channel_id=1, source_target_pairs={{0,8},{8,0},{16,24},{24,16},{1,9},{9,1},{17,25},{25,17},{2,10},{10... | collective-permute-start | bytes 786440 | tf_op jit(solution)/shard_map/ppermute | solution.py:520
  180.6 14.8 %collective-permute-start.7 = (bf16[128,1024]{1,0:T(8,128)(2,1)}, bf16[128,1024]{1,0:T(8,128)(2,1)}, u32[]{:S(2)}, u32[]{:S(2)}) collective-permute-start(bf16[128,1024]{1,0:T(8,128)(2,1)} %get-tuple-element.49), channel_id=1, source_target_pairs={{0,16},{8,24},{16,0},{24,8},{1,17},{9,25},{17,1},{25,9},{2,18},{10... | collective-permute-start | bytes 786440 | tf_op jit(solution)/shard_map/ppermute | solution.py:520
  181.4 18.2 %collective-permute-start.8 = (bf16[128,1024]{1,0:T(8,128)(2,1)}, bf16[128,1024]{1,0:T(8,128)(2,1)}, u32[]{:S(2)}, u32[]{:S(2)}) collective-permute-start(bf16[128,1024]{1,0:T(8,128)(2,1)} %get-tuple-element.50), channel_id=1, source_target_pairs={{0,24},{8,16},{16,8},{24,0},{1,25},{9,17},{17,9},{25,1},{2,26},{10... | collective-permute-start | bytes 786440 | tf_op jit(solution)/shard_map/ppermute | solution.py:520
  191.5 45.9 %collective-permute-start = (bf16[128,2048]{1,0:T(8,128)(2,1)}, bf16[128,2048]{1,0:T(8,128)(2,1)}, u32[]{:S(2)}, u32[]{:S(2)}) collective-permute-start(bf16[128,2048]{1,0:T(8,128)(2,1)} %get-tuple-element.42), channel_id=1, source_target_pairs={{0,8},{8,0},{16,24},{24,16},{1,9},{9,1},{17,25},{25,17},{2,10},{10... | collective-permute-start | bytes 1572872 | tf_op jit(solution)/shard_map/ppermute | solution.py:520
  192.0 46.5 %collective-permute-start.1 = (bf16[128,2048]{1,0:T(8,128)(2,1)}, bf16[128,2048]{1,0:T(8,128)(2,1)}, u32[]{:S(2)}, u32[]{:S(2)}) collective-permute-start(bf16[128,2048]{1,0:T(8,128)(2,1)} %get-tuple-element.43), channel_id=1, source_target_pairs={{0,16},{8,24},{16,0},{24,8},{1,17},{9,25},{17,1},{25,9},{2,18},{10... | collective-permute-start | bytes 1572872 | tf_op jit(solution)/shard_map/ppermute | solution.py:520
  193.7 46.6 %collective-permute-start.2 = (bf16[128,2048]{1,0:T(8,128)(2,1)}, bf16[128,2048]{1,0:T(8,128)(2,1)}, u32[]{:S(2)}, u32[]{:S(2)}) collective-permute-start(bf16[128,2048]{1,0:T(8,128)(2,1)} %get-tuple-element.44), channel_id=1, source_target_pairs={{0,24},{8,16},{16,8},{24,0},{1,25},{9,17},{17,9},{25,1},{2,26},{10... | collective-permute-start | bytes 1572872 | tf_op jit(solution)/shard_map/ppermute | solution.py:520
  195.3 37.1 %collective-permute-start.4 = (bf16[128,1024]{1,0:T(8,128)(2,1)}, bf16[128,1024]{1,0:T(8,128)(2,1)}, u32[]{:S(2)}, u32[]{:S(2)}) collective-permute-start(bf16[128,1024]{1,0:T(8,128)(2,1)} %get-tuple-element.46), channel_id=1, source_target_pairs={{0,16},{8,24},{16,0},{24,8},{1,17},{9,25},{17,1},{25,9},{2,18},{10... | collective-permute-start | bytes 786440 | tf_op jit(solution)/shard_map/ppermute | solution.py:520
  199.6 32.9 %collective-permute-start.5 = (bf16[128,1024]{1,0:T(8,128)(2,1)}, bf16[128,1024]{1,0:T(8,128)(2,1)}, u32[]{:S(2)}, u32[]{:S(2)}) collective-permute-start(bf16[128,1024]{1,0:T(8,128)(2,1)} %get-tuple-element.47), channel_id=1, source_target_pairs={{0,24},{8,16},{16,8},{24,0},{1,25},{9,17},{17,9},{25,1},{2,26},{10... | collective-permute-start | bytes 786440 | tf_op jit(solution)/shard_map/ppermute | solution.py:520
  235.4 10.7 %collective-permute-start.12 = (bf16[128,1024]{1,0:T(8,128)(2,1)}, bf16[128,1024]{1,0:T(8,128)(2,1)}, u32[]{:S(2)}, u32[]{:S(2)}) collective-permute-start(bf16[128,1024]{1,0:T(8,128)(2,1)} %get-tuple-element.58), channel_id=1, source_target_pairs={{0,8},{8,0},{16,24},{24,16},{1,9},{9,1},{17,25},{25,17},{2,10},{10... | collective-permute-start | bytes 786440 | tf_op jit(solution)/shard_map/ppermute | solution.py:520
  236.7 13.8 %collective-permute-start.15 = (bf16[128,1024]{1,0:T(8,128)(2,1)}, bf16[128,1024]{1,0:T(8,128)(2,1)}, u32[]{:S(2)}, u32[]{:S(2)}) collective-permute-start(bf16[128,1024]{1,0:T(8,128)(2,1)} %get-tuple-element.61), channel_id=1, source_target_pairs={{0,8},{8,0},{16,24},{24,16},{1,9},{9,1},{17,25},{25,17},{2,10},{10... | collective-permute-start | bytes 786440 | tf_op jit(solution)/shard_map/ppermute | solution.py:520
  237.4 14.4 %collective-permute-start.16 = (bf16[128,1024]{1,0:T(8,128)(2,1)}, bf16[128,1024]{1,0:T(8,128)(2,1)}, u32[]{:S(2)}, u32[]{:S(2)}) collective-permute-start(bf16[128,1024]{1,0:T(8,128)(2,1)} %get-tuple-element.62), channel_id=1, source_target_pairs={{0,16},{8,24},{16,0},{24,8},{1,17},{9,25},{17,1},{25,9},{2,18},{10... | collective-permute-start | bytes 786440 | tf_op jit(solution)/shard_map/ppermute | solution.py:520
  238.5 18.2 %collective-permute-start.17 = (bf16[128,1024]{1,0:T(8,128)(2,1)}, bf16[128,1024]{1,0:T(8,128)(2,1)}, u32[]{:S(2)}, u32[]{:S(2)}) collective-permute-start(bf16[128,1024]{1,0:T(8,128)(2,1)} %get-tuple-element.63), channel_id=1, source_target_pairs={{0,24},{8,16},{16,8},{24,0},{1,25},{9,17},{17,9},{25,1},{2,26},{10... | collective-permute-start | bytes 786440 | tf_op jit(solution)/shard_map/ppermute | solution.py:520
  240.2 37.1 %collective-permute-start.13 = (bf16[128,1024]{1,0:T(8,128)(2,1)}, bf16[128,1024]{1,0:T(8,128)(2,1)}, u32[]{:S(2)}, u32[]{:S(2)}) collective-permute-start(bf16[128,1024]{1,0:T(8,128)(2,1)} %get-tuple-element.59), channel_id=1, source_target_pairs={{0,16},{8,24},{16,0},{24,8},{1,17},{9,25},{17,1},{25,9},{2,18},{10... | collective-permute-start | bytes 786440 | tf_op jit(solution)/shard_map/ppermute | solution.py:520
  246.1 31.2 %collective-permute-start.14 = (bf16[128,1024]{1,0:T(8,128)(2,1)}, bf16[128,1024]{1,0:T(8,128)(2,1)}, u32[]{:S(2)}, u32[]{:S(2)}) collective-permute-start(bf16[128,1024]{1,0:T(8,128)(2,1)} %get-tuple-element.60), channel_id=1, source_target_pairs={{0,24},{8,16},{16,8},{24,0},{1,25},{9,17},{17,9},{25,1},{2,26},{10... | collective-permute-start | bytes 786440 | tf_op jit(solution)/shard_map/ppermute | solution.py:520
  250.5 29.1 %collective-permute-start.9 = (bf16[128,2048]{1,0:T(8,128)(2,1)}, bf16[128,2048]{1,0:T(8,128)(2,1)}, u32[]{:S(2)}, u32[]{:S(2)}) collective-permute-start(bf16[128,2048]{1,0:T(8,128)(2,1)} %get-tuple-element.55), channel_id=1, source_target_pairs={{0,8},{8,0},{16,24},{24,16},{1,9},{9,1},{17,25},{25,17},{2,10},{10... | collective-permute-start | bytes 1572872 | tf_op jit(solution)/shard_map/ppermute | solution.py:520
  251.8 32.8 %collective-permute-start.10 = (bf16[128,2048]{1,0:T(8,128)(2,1)}, bf16[128,2048]{1,0:T(8,128)(2,1)}, u32[]{:S(2)}, u32[]{:S(2)}) collective-permute-start(bf16[128,2048]{1,0:T(8,128)(2,1)} %get-tuple-element.56), channel_id=1, source_target_pairs={{0,16},{8,24},{16,0},{24,8},{1,17},{9,25},{17,1},{25,9},{2,18},{10... | collective-permute-start | bytes 1572872 | tf_op jit(solution)/shard_map/ppermute | solution.py:520
  256.7 28.0 %collective-permute-start.11 = (bf16[128,2048]{1,0:T(8,128)(2,1)}, bf16[128,2048]{1,0:T(8,128)(2,1)}, u32[]{:S(2)}, u32[]{:S(2)}) collective-permute-start(bf16[128,2048]{1,0:T(8,128)(2,1)} %get-tuple-element.57), channel_id=1, source_target_pairs={{0,24},{8,16},{16,8},{24,0},{1,25},{9,17},{17,9},{25,1},{2,26},{10... | collective-permute-start | bytes 1572872 | tf_op jit(solution)/shard_map/ppermute | solution.py:520
